TPU v7x, 32 devices: a whole 2x2x4 slice. The times are simulated.
32 devices in a mesh: seq: 4 (over y, x), head: 8 (over z, core).
Axes of the slice: x: 2, y: 2, z: 4, core: 2. Of those that a mesh axis runs over, the one named last changes fastest.
Arguments:
- inputs: bfloat16 [4096, 6144], P('seq', 'head'), may hold values from -6 to 6
- projection: bfloat16 [6144, 3, 4096], P('seq', None, 'head'), may hold values from -0.078125 to 0.078125
- cotangent: bfloat16 [4096, 4096], P('seq', 'head'), may hold values from -0.3125 to 0.3125
- log_decay: float32 [32, 4096], P('head', 'seq'), may hold values from -0.7 to 0
- document_starts: int32 [4], replicated, may hold values from 0 to 3328, as said below
Outputs:
- input_gradient: bfloat16 [4096, 6144], P('seq', 'head')
- weight_gradient: bfloat16 [6144, 3, 4096], P('seq', None, 'head')
Inputs may be any that keep to these rules, and one draw needn't show every extreme that they name: `document_starts`: strictly increasing; the first is 0 and the last is (3) * 1024 + 256.
All inputs are finite; a program needn't handle non-finite values.
Results may differ from a plain program's by a relative error of at most 0.02.
Values may be sent and summed in bfloat16 or wider, within the bound.
A program may use at most 192 MiB of HBM per device.

v0:
```python
import jax
import jax.numpy as jnp
from jax import lax
from jax.sharding import PartitionSpec as P

HEAD_DIM = 128
BLOCK = 256


def prefix(array, axis, combine, identity, reverse):
    length, place = (lax.axis_size(axis), lax.axis_index(axis))
    everything = jax.tree.map(
        lambda part, kind: lax.all_gather(part.astype(kind), axis),
        array,
        (jnp.bfloat16, jnp.bfloat16),
    )
    start = jax.tree.map(
        lambda part, zero: jnp.broadcast_to(jnp.asarray(zero, part.dtype), part.shape),
        array,
        identity,
    )

    def turn(k, before):
        at = length - 1 - k if reverse else k
        reached = at > place if reverse else at < place
        new = combine(
            before, jax.tree.map(lambda part, own: part[at].astype(own.dtype), everything, array)
        )
        return jax.tree.map(lambda a, b: jnp.where(reached, a, b), new, before)

    return lax.fori_loop(0, length, turn, start)


def silu_slope(point):
    sigma = jax.nn.sigmoid(point)
    return sigma * (1.0 + point * (1.0 - sigma))


def block_factors(decay_sum, doc_index, doc_begin):
    inside = jnp.arange(doc_index.shape[-1], dtype=jnp.int32)
    causal = inside[:, None] >= inside[None, :]
    same_doc = (doc_index[:, :, None] == doc_index[:, None, :]) & causal[None]
    spread = jnp.minimum(decay_sum[..., :, None] - decay_sum[..., None, :], 0.0)
    pair_weight = jnp.where(same_doc[None], jnp.exp(spread), 0.0)
    to_end = jnp.where(
        (doc_index == doc_index[:, -1:])[None], jnp.exp(decay_sum[..., -1:] - decay_sum), 0.0
    )
    began_flag = doc_index == doc_index[:, :1] - doc_begin[:, :1]
    from_start = jnp.where(began_flag[None], jnp.exp(decay_sum), 0.0)
    return (pair_weight, to_end, from_start, from_start[..., -1])


def combine_states(earlier, later):
    return (earlier[0] * later[0], later[0][:, None, None] * earlier[1] + later[1])


def body(inputs, projection, cotangent, log_decay, document_starts):
    tokens = inputs.shape[0]
    heads_here = log_decay.shape[0]
    local_cols = cotangent.shape[1]
    blocks = tokens // BLOCK
    query_scale = HEAD_DIM ** (-0.5)
    features = lax.all_gather(inputs, "head", axis=1, tiled=True)
    weights_all = lax.all_gather(projection, "seq", axis=0, tiled=True)
    projected = jnp.einsum("td,dkc->tkc", features, weights_all, preferred_element_type=jnp.float32)
    queries = (jax.nn.silu(projected[:, 0]) * query_scale).astype(jnp.bfloat16)
    keys = jax.nn.silu(projected[:, 1]).astype(jnp.bfloat16)
    values = projected[:, 2].astype(jnp.bfloat16)

    def split_blocks(table):
        return table.reshape(blocks, BLOCK, heads_here, HEAD_DIM).transpose(2, 0, 1, 3)

    def merge_blocks(table):
        return table.transpose(1, 2, 0, 3).reshape(tokens, local_cols)

    queries_b = split_blocks(queries)
    keys_b = split_blocks(keys)
    values_b = split_blocks(values)
    upstream = split_blocks(cotangent)
    offset = lax.axis_index("seq") * tokens
    positions = offset + jnp.arange(tokens, dtype=jnp.int32)
    doc_index = (
        jnp.sum((document_starts[None, :] <= positions[:, None]).astype(jnp.int32), axis=1) - 1
    )
    doc_begin = jnp.any(document_starts[None, :] == positions[:, None], axis=1).astype(jnp.int32)
    decay_sum = jnp.cumsum(log_decay.reshape(heads_here, blocks, BLOCK), axis=-1)
    pair_weight, to_end, from_start, block_decay = block_factors(
        decay_sum, doc_index.reshape(blocks, BLOCK), doc_begin.reshape(blocks, BLOCK)
    )
    keys_weighted = (keys_b.astype(jnp.float32) * to_end[..., None]).astype(jnp.bfloat16)
    queries_weighted = (queries_b.astype(jnp.float32) * from_start[..., None]).astype(jnp.bfloat16)
    key_state = jnp.einsum(
        "hbse,hbsf->hbef", keys_weighted, values_b, preferred_element_type=jnp.float32
    )
    query_state = jnp.einsum(
        "hbte,hbtf->hbef", queries_weighted, upstream, preferred_element_type=jnp.float32
    )

    def local_step(carry, item):
        return (combine_states(carry, item), carry)

    ones = jnp.ones((heads_here,), jnp.float32)
    empty = jnp.zeros((heads_here, HEAD_DIM, HEAD_DIM), jnp.float32)
    (device_decay, device_keys), (prior_decay, prior_keys) = lax.scan(
        local_step, (ones, empty), (block_decay.T, key_state.swapaxes(0, 1))
    )
    (device_decay_back, device_query), (later_decay, later_query) = lax.scan(
        local_step, (ones, empty), (block_decay.T, query_state.swapaxes(0, 1)), reverse=True
    )
    forward_in = prefix((device_decay, device_keys), "seq", combine_states, (ones, empty), False)[1]
    backward_in = prefix(
        (device_decay_back, device_query), "seq", combine_states, (ones, empty), True
    )[1]
    state_before = (
        (prior_decay[:, :, None, None] * forward_in[None] + prior_keys)
        .swapaxes(0, 1)
        .astype(jnp.bfloat16)
    )
    state_after = (
        (later_decay[:, :, None, None] * backward_in[None] + later_query)
        .swapaxes(0, 1)
        .astype(jnp.bfloat16)
    )
    query_key = (
        jnp.einsum("hbte,hbse->hbts", queries_b, keys_b, preferred_element_type=jnp.float32)
        * pair_weight
    ).astype(jnp.bfloat16)
    value_score = (
        jnp.einsum("hbtf,hbsf->hbts", upstream, values_b, preferred_element_type=jnp.float32)
        * pair_weight
    ).astype(jnp.bfloat16)
    query_gradient = jnp.einsum(
        "hbts,hbse->hbte", value_score, keys_b, preferred_element_type=jnp.float32
    ) + from_start[..., None] * jnp.einsum(
        "hbtf,hbef->hbte", upstream, state_before, preferred_element_type=jnp.float32
    )
    key_gradient = jnp.einsum(
        "hbts,hbte->hbse", value_score, queries_b, preferred_element_type=jnp.float32
    ) + to_end[..., None] * jnp.einsum(
        "hbsf,hbef->hbse", values_b, state_after, preferred_element_type=jnp.float32
    )
    value_gradient = jnp.einsum(
        "hbts,hbtf->hbsf", query_key, upstream, preferred_element_type=jnp.float32
    ) + to_end[..., None] * jnp.einsum(
        "hbse,hbef->hbsf", keys_b, state_after, preferred_element_type=jnp.float32
    )
    project_gradient = jnp.stack(
        [
            merge_blocks(query_gradient) * silu_slope(projected[:, 0]) * query_scale,
            merge_blocks(key_gradient) * silu_slope(projected[:, 1]),
            merge_blocks(value_gradient),
        ],
        axis=1,
    ).astype(jnp.bfloat16)
    partial_value = jnp.einsum(
        "tkc,dkc->td", project_gradient, weights_all, preferred_element_type=jnp.float32
    )
    input_gradient = lax.psum_scatter(
        partial_value.astype(jnp.bfloat16), "head", scatter_dimension=1, tiled=True
    )
    weight_gradient = lax.psum_scatter(
        jnp.einsum(
            "td,tkc->dkc", features, project_gradient, preferred_element_type=jnp.float32
        ).astype(jnp.bfloat16),
        "seq",
        scatter_dimension=0,
        tiled=True,
    )
    return (input_gradient, weight_gradient)


def solution(mesh):
    placed = (P("seq", "head"), P("seq", None, "head"), P("seq", "head"), P("head", "seq"), P())
    return jax.shard_map(
        body,
        mesh=mesh,
        in_specs=placed,
        out_specs=(P("seq", "head"), P("seq", None, "head")),
        check_vma=False,
    )
```

profile of v0, /device:TPU:0, one launch (start us, length us, event | category | flops | bytes accessed | tf_op | source)
XLA Modules:
  0.0 778.4 jit_solution(1221711399798025846)
XLA Ops:
  8.8 4.8 reduce-window.6
  19.3 109.7 %all-gather.7.cloned.1.call-done = bf16[1024,6144]{1,0:T(8,128)(2,1)} async-done(((bf16[1024,768]{1,0:T(8,128)(2,1)}), bf16[1024,6144]{1,0:T(8,128)(2,1)}) %all-gather.7.cloned.1.call-update) | async-done | bytes 12582928 | tf_op jit(solution)/shard_map/all_gather | solution.py:63
  129.1 175.4 %all-gather.9.cloned.1.call-done = bf16[6144,3,512]{2,0,1:T(8,128)(2,1)} async-done(((bf16[1536,3,512]{2,0,1:T(8,128)(2,1)}), bf16[6144,3,512]{2,0,1:T(8,128)(2,1)}) %all-gather.9.cloned.1.call-update) | async-done | bytes 18874384 | tf_op jit(solution)/shard_map/all_gather | solution.py:64
  304.5 23.7 %fusion.9 = f32[1024,3,512]{2,0,1:T(8,128)S(1)} fusion(bf16[6144,3,512]{2,0,1:T(8,128)(2,1)} %all-gather.9.cloned.1.call-done, bf16[1024,6144]{1,0:T(8,128)(2,1)} %all-gather.7.cloned.1.call-done), kind=kOutput, calls=%fused_computation.23 | convolution fusion | flops 19327352832 | bytes 37748736 | tf_op jit(solution)/shard_map/td,dkc->tkc/dot_general | solution.py:65
  328.2 2.0 fusion.57
  334.3 2.1 multiply_convert_fusion.6
  336.4 3.0 squeeze.59
  339.5 3.9 convolution_bitcast_fusion
  343.5 4.6 while.70
  350.4 5.5 fusion.16
  355.9 3.7 fusion.11
  359.7 2.4 convolution_bitcast_fusion.1
  363.2 7.5 while.68
  370.7 4.5 fusion.20
  375.6 3.7 fusion.26
  379.3 8.9 %all-reduce.2 = (bf16[16]{0:T(256)(128)(2,1)S(1)}, bf16[16]{0:T(256)(128)(2,1)S(1)}) all-reduce(bf16[16]{0:T(256)(128)(2,1)S(1)} %dynamic-update-slice.1, bf16[16]{0:T(256)(128)(2,1)S(1)} %dynamic-update-slice), channel_id=4, replica_groups=mesh['seq'=4,'head'=8] {'seq'}, use_global_device_ids=true, to_apply=%add.1 | all-reduce | flops 32 | bytes 128
  388.3 11.3 %all-gather.3 = bf16[16,128,128]{2,1,0:T(8,128)(2,1)} all-gather(bf16[4,128,128]{2,1,0:T(8,128)(2,1)S(1)} %convert_element_type.142), channel_id=5, replica_groups=mesh['seq'=4,'head'=8] {'seq'}, dimensions={0}, use_global_device_ids=true | all-gather | bytes 655360 | tf_op jit(solution)/shard_map/all_gather | solution.py:13
  399.6 4.2 while.71
  403.8 2.4 fusion.13
  408.4 9.3 %all-gather.1 = bf16[16,128,128]{2,1,0:T(8,128)(2,1)S(1)} all-gather(bf16[4,128,128]{2,1,0:T(8,128)(2,1)S(1)} %convert_element_type.135), channel_id=3, replica_groups=mesh['seq'=4,'head'=8] {'seq'}, dimensions={0}, use_global_device_ids=true | all-gather | bytes 655360 | tf_op jit(solution)/shard_map/all_gather | solution.py:13
  418.3 2.7 fusion.15
  421.1 2.7 copy.160
  423.7 3.1 reshape.184
  426.9 2.0 fusion.14
  428.9 2.7 copy.169
  431.6 3.2 reshape.185
  434.8 4.4 multiply_convert_fusion.4
  440.2 28.6 %convert_bitcast_fusion = bf16[6144,3,512]{0,2,1:T(8,128)(2,1)} fusion(bf16[1024,6144]{1,0:T(8,128)(2,1)} %all-gather.7.cloned.1.call-done, bf16[1024,1,512]{2,0,1:T(8,128)(2,1)S(1)} %copy-done.9, bf16[1024,1,512]{2,0,1:T(8,128)(2,1)S(1)} %get-tuple-element.645, bf16[1024,1,512]{2,0,1:T(8,128)(2,1)S(1)} %get-tuple-element.644), kind=kOutput, calls=%fused_computation.21 | convolution fusion | flops 19339935744 | bytes 34603008 | tf_op jit(solution)/shard_map/td,tkc->dkc/dot_general | solution.py:162
  470.3 24.9 %bitcast_convert_fusion.2 = bf16[1024,6144]{1,0:T(8,128)(2,1)} fusion(bf16[6144,3,512]{2,0,1:T(8,128)(2,1)} %all-gather.9.cloned.1.call-done, bf16[1024,1,512]{2,0,1:T(8,128)(2,1)S(1)} %copy-done.10, bf16[1024,1,512]{2,0,1:T(8,128)(2,1)S(1)} %copy-done.7, bf16[1024,1,512]{2,0,1:T(8,128)(2,1)S(1)} %get-tuple-element.644), kind=kOutput, calls=%fused_computation.20 | convolution fusion | flops 19336790016 | bytes 34603008 | tf_op jit(solution)/shard_map/tkc,dkc->td/dot_general | solution.py:155
  495.3 144.5 %reduce-scatter.5.cloned.1.call-done = bf16[1536,3,512]{0,2,1:T(8,128)(2,1)} async-done(((bf16[6144,3,512]{0,2,1:T(8,128)(2,1)}), bf16[1536,3,512]{0,2,1:T(8,128)(2,1)}) %reduce-scatter.5.cloned.1.call-update) | async-done | bytes 4718608 | tf_op jit(solution)/shard_map/reduce_scatter | solution.py:161
  639.8 6.6 copy.174
  646.4 125.4 %reduce-scatter.3.cloned.1.call-done = bf16[1024,768]{1,0:T(8,128)(2,1)} async-done(((bf16[1024,6144]{1,0:T(8,128)(2,1)}), bf16[1024,768]{1,0:T(8,128)(2,1)}) %reduce-scatter.3.cloned.1.call-update) | async-done | bytes 1572880 | tf_op jit(solution)/shard_map/reduce_scatter | solution.py:158
  (141 shorter events, 36.1 us)
Async XLA Ops:
  7.2 121.9 %all-gather.7.cloned.1.call-start = ((), (), s32[]{:S(2)}) async-start(), calls=%async_computation.2 | async-start | bytes 14155776 | tf_op jit(solution)/shard_map/all_gather | solution.py:63
  7.9 0.9 copy-start.11
  7.9 6.2 copy-start.12
  7.9 6.3 copy-start.8
  7.9 296.5 %all-gather.9.cloned.1.call-start = ((), (), s32[]{:S(2)}) async-start(), calls=%async_computation.3 | async-start | bytes 23592960 | tf_op jit(solution)/shard_map/all_gather | solution.py:64
  8.7 631.1 %reduce-scatter.5.cloned.1.call-start = ((), (), s32[]{:S(2)}) async-start(), calls=%async_computation.5 | async-start | bytes 23592960 | tf_op jit(solution)/shard_map/reduce_scatter | solution.py:161
  15.4 2.4 copy-start.13
  328.2 3.2 copy-start
  336.4 3.0 copy-start.4
  348.1 1.0 copy-start.1
  408.4 10.0 %copy-start.5 = (bf16[4,256,4,128]{3,2,1,0:T(4,128)(2,1)S(1)}, bf16[4,256,4,128]{3,2,1,0:T(4,128)(2,1)}, u32[]{:S(2)}) copy-start(bf16[4,256,4,128]{3,2,1,0:T(4,128)(2,1)} %reshape.181) | copy-start | bytes 3145732
  423.7 3.1 copy-start.2
  431.6 3.2 copy-start.3
  434.8 5.4 copy-start.9
  439.3 1.0 copy-start.6
  468.8 1.2 copy-start.7
  468.8 1.5 copy-start.10
  468.8 303.0 %reduce-scatter.3.cloned.1.call-start = ((), (), s32[]{:S(2)}) async-start(), calls=%async_computation.4 | async-start | bytes 14155776 | tf_op jit(solution)/shard_map/reduce_scatter | solution.py:158
Sparse Core Ops, SparseCore 0:
  9.6 119.4 all-gather.6
  130.9 173.4 all-gather.8
  468.9 170.7 reduce-scatter.4
  642.6 129.1 reduce-scatter.2
where the time goes:
time: 779 us; the launch traced here: 778 us
  waiting for transfers between devices  557 us (72%)
  matrix products  108 us (14%)
  local copies, waits for them, and re-layouts  40 us (5%)
  blocking collectives  29.5 us (4%)
  other arithmetic  28.8 us (4%)
  between operations  14.8 us (2%)
    all_gather x1, waiting for transfers between devices, body(): weights_all = lax.all_gather(projection, 'seq', axis=0, tiled=True)  175 us
    reduce_scatter x1, waiting for transfers between devices, body(): lax.psum_scatter(jnp.einsum('td,tkc->dkc', features, project_gradient, pr...  145 us
    reduce_scatter x1, waiting for transfers between devices, body(): lax.psum_scatter(partial_value.astype(jnp.bfloat16), 'head', scatter_dime...  125 us
    all_gather x1, waiting for transfers between devices, body(): features = lax.all_gather(inputs, 'head', axis=1, tiled=True)  110 us
    dot_general x1, matrix products, body(): jnp.einsum('td,tkc->dkc', features, project_gradient, preferred_element_t...  28.6 us
    dot_general x1, matrix products, body(): jnp.einsum('tkc,dkc->td', project_gradient, weights_all, preferred_elemen...  24.9 us
    dot_general x1, matrix products, body(): jnp.einsum('td,dkc->tkc', features, weights_all, preferred_element_type=j...  23.7 us
    all_gather x2, blocking collectives, prefix(): lax.all_gather(part.astype(kind), axis)  20.6 us
  transfers between devices with their start and end apart: 4, of which 4 were waited for; matrix products, arithmetic and copies ran while one was open for 5% of the time, Pallas kernels for 0%

commit v1 on v0

--- a/solution.py
+++ b/solution.py
@@ -7,28 +7,79 @@
 BLOCK = 256
 
 
-def prefix(array, axis, combine, identity, reverse):
-    length, place = (lax.axis_size(axis), lax.axis_index(axis))
-    everything = jax.tree.map(
-        lambda part, kind: lax.all_gather(part.astype(kind), axis),
-        array,
-        (jnp.bfloat16, jnp.bfloat16),
-    )
-    start = jax.tree.map(
-        lambda part, zero: jnp.broadcast_to(jnp.asarray(zero, part.dtype), part.shape),
-        array,
-        identity,
-    )
-
-    def turn(k, before):
+def hop(array, axis, flip):
+    return lax.ppermute(array, axis, [(i, i ^ flip) for i in range(lax.axis_size(axis))])
+
+
+def gather_states(packed, axis):
+    length = lax.axis_size(axis)
+    if length != 4:
+        return lax.all_gather(packed, axis)
+    place = lax.axis_index(axis)
+    parts = [packed] + [hop(packed, axis, flip) for flip in range(1, length)]
+    rows = []
+    for at in range(length):
+        row = parts[0]
+        for flip in range(1, length):
+            row = jnp.where(place == (at ^ flip), parts[flip], row)
+        rows.append(row)
+    return rows
+
+
+def combine_devices(states, decays, place, reverse):
+    length = len(decays)
+    total = jnp.zeros_like(states[0])
+    for k in range(length):
         at = length - 1 - k if reverse else k
         reached = at > place if reverse else at < place
-        new = combine(
-            before, jax.tree.map(lambda part, own: part[at].astype(own.dtype), everything, array)
+        total = jnp.where(reached, decays[at][:, None, None] * total + states[at], total)
+    return total
+
+
+def gather_rows(part, axis):
+    length, place, rows = (lax.axis_size(axis), lax.axis_index(axis), part.shape[1])
+    if length != 4:
+        whole = lax.all_gather(part, axis, axis=1, tiled=True)
+        return [(0, 0, whole)]
+    half = rows // 2
+    low, high = part[:, :half], part[:, half:]
+    x_high = hop(high, axis, 1)
+    y_low = hop(low, axis, 2)
+    x_low = hop(low, axis, 1)
+    y_high = hop(high, axis, 2)
+    d_low = hop(y_low, axis, 1)
+    d_high = hop(x_high, axis, 2)
+    return [
+        (place, 0, low),
+        (place, half, high),
+        (place ^ 1, half, x_high),
+        (place ^ 2, 0, y_low),
+        (place ^ 1, 0, x_low),
+        (place ^ 2, half, y_high),
+        (place ^ 3, 0, d_low),
+        (place ^ 3, half, d_high),
+    ]
+
+
+def scatter_rows(partial, axis, rows):
+    length, place = (lax.axis_size(axis), lax.axis_index(axis))
+    if length != 4:
+        return lax.psum_scatter(
+            partial(0, 0, rows * length), axis, scatter_dimension=1, tiled=True
         )
-        return jax.tree.map(lambda a, b: jnp.where(reached, a, b), new, before)
-
-    return lax.fori_loop(0, length, turn, start)
+    half = rows // 2
+
+    def add(*terms):
+        return sum(term.astype(jnp.float32) for term in terms).astype(jnp.bfloat16)
+
+    far_low = hop(partial(place ^ 3, 0, half), axis, 1)
+    far_high = hop(partial(place ^ 3, half, half), axis, 2)
+    x_low = hop(partial(place ^ 1, 0, half), axis, 1)
+    y_high = hop(partial(place ^ 2, half, half), axis, 2)
+    x_high = hop(add(partial(place ^ 1, half, half), far_high), axis, 1)
+    y_low = hop(add(partial(place ^ 2, 0, half), far_low), axis, 2)
+    own_low, own_high = partial(place, 0, half), partial(place, half, half)
+    return jnp.concatenate([add(own_low, x_low, y_low), add(own_high, x_high, y_high)], axis=1)
 
 
 def silu_slope(point):
@@ -50,6 +101,14 @@
     return (pair_weight, to_end, from_start, from_start[..., -1])
 
 
+def block_pair(decay):
+    high = decay.astype(jnp.bfloat16)
+    low = (decay - high.astype(jnp.float32)).astype(jnp.bfloat16)
+    pair = jnp.stack([high, low], axis=1)
+    slab = jnp.pad(pair, ((0, HEAD_DIM - pair.shape[0]), (0, HEAD_DIM - 2)))
+    return slab[None]
+
+
 def combine_states(earlier, later):
     return (earlier[0] * later[0], later[0][:, None, None] * earlier[1] + later[1])
 
@@ -61,11 +120,24 @@
     blocks = tokens // BLOCK
     query_scale = HEAD_DIM ** (-0.5)
     features = lax.all_gather(inputs, "head", axis=1, tiled=True)
-    weights_all = lax.all_gather(projection, "seq", axis=0, tiled=True)
-    projected = jnp.einsum("td,dkc->tkc", features, weights_all, preferred_element_type=jnp.float32)
-    queries = (jax.nn.silu(projected[:, 0]) * query_scale).astype(jnp.bfloat16)
-    keys = jax.nn.silu(projected[:, 1]).astype(jnp.bfloat16)
-    values = projected[:, 2].astype(jnp.bfloat16)
+    rows = projection.shape[0]
+    blocks_w = gather_rows(projection.transpose(1, 0, 2), "seq")
+
+    def feature_rows(owner, first, count):
+        return lax.dynamic_slice_in_dim(features, owner * rows + first, count, axis=1)
+
+    projected = sum(
+        jnp.einsum(
+            "td,kdc->ktc",
+            feature_rows(owner, first, block.shape[1]),
+            block,
+            preferred_element_type=jnp.float32,
+        )
+        for owner, first, block in blocks_w
+    )
+    queries = (jax.nn.silu(projected[0]) * query_scale).astype(jnp.bfloat16)
+    keys = jax.nn.silu(projected[1]).astype(jnp.bfloat16)
+    values = projected[2].astype(jnp.bfloat16)
 
     def split_blocks(table):
         return table.reshape(blocks, BLOCK, heads_here, HEAD_DIM).transpose(2, 0, 1, 3)
@@ -107,10 +179,21 @@
     (device_decay_back, device_query), (later_decay, later_query) = lax.scan(
         local_step, (ones, empty), (block_decay.T, query_state.swapaxes(0, 1)), reverse=True
     )
-    forward_in = prefix((device_decay, device_keys), "seq", combine_states, (ones, empty), False)[1]
-    backward_in = prefix(
-        (device_decay_back, device_query), "seq", combine_states, (ones, empty), True
-    )[1]
+    place = lax.axis_index("seq")
+    rough = block_pair(device_decay)
+    packed = jnp.concatenate(
+        [device_keys.astype(jnp.bfloat16), device_query.astype(jnp.bfloat16), rough]
+    )
+    everything = gather_states(packed, "seq")
+    everything = [everything[k].astype(jnp.float32) for k in range(lax.axis_size("seq"))]
+    decays = [
+        part[2 * heads_here, :heads_here, 0] + part[2 * heads_here, :heads_here, 1]
+        for part in everything
+    ]
+    forward_in = combine_devices([part[:heads_here] for part in everything], decays, place, False)
+    backward_in = combine_devices(
+        [part[heads_here : 2 * heads_here] for part in everything], decays, place, True
+    )
     state_before = (
         (prior_decay[:, :, None, None] * forward_in[None] + prior_keys)
         .swapaxes(0, 1)
@@ -146,26 +229,30 @@
     )
     project_gradient = jnp.stack(
         [
-            merge_blocks(query_gradient) * silu_slope(projected[:, 0]) * query_scale,
-            merge_blocks(key_gradient) * silu_slope(projected[:, 1]),
+            merge_blocks(query_gradient) * silu_slope(projected[0]) * query_scale,
+            merge_blocks(key_gradient) * silu_slope(projected[1]),
             merge_blocks(value_gradient),
         ],
-        axis=1,
+        axis=0,
     ).astype(jnp.bfloat16)
-    partial_value = jnp.einsum(
-        "tkc,dkc->td", project_gradient, weights_all, preferred_element_type=jnp.float32
-    )
-    input_gradient = lax.psum_scatter(
-        partial_value.astype(jnp.bfloat16), "head", scatter_dimension=1, tiled=True
-    )
-    weight_gradient = lax.psum_scatter(
-        jnp.einsum(
-            "td,tkc->dkc", features, project_gradient, preferred_element_type=jnp.float32
-        ).astype(jnp.bfloat16),
-        "seq",
-        scatter_dimension=0,
-        tiled=True,
-    )
+    def weight_partial(owner, first, count):
+        return jnp.einsum(
+            "td,ktc->kdc",
+            feature_rows(owner, first, count),
+            project_gradient,
+            preferred_element_type=jnp.float32,
+        ).astype(jnp.bfloat16)
+
+    partial_value = jnp.zeros((tokens, features.shape[1]), jnp.bfloat16)
+    for owner, first, block in blocks_w:
+        piece = jnp.einsum(
+            "ktc,kdc->td", project_gradient, block, preferred_element_type=jnp.float32
+        ).astype(jnp.bfloat16)
+        partial_value = lax.dynamic_update_slice_in_dim(
+            partial_value, piece, owner * rows + first, axis=1
+        )
+    input_gradient = lax.psum_scatter(partial_value, "head", scatter_dimension=1, tiled=True)
+    weight_gradient = scatter_rows(weight_partial, "seq", rows).transpose(1, 0, 2)
     return (input_gradient, weight_gradient)
 
 

time: 779 us -> 538 us (0.69); the launches traced: 778 us -> 528 us
  waiting for transfers between devices: 557 us -> 241 us
  matrix products: 108 us -> 160 us
  blocking collectives: 29.5 us -> 0 us
  starting transfers between devices: 0.16 us -> 18.8 us
  local copies, waits for them, and re-layouts: 40 us -> 55.5 us
  other arithmetic: 28.8 us -> 37.3 us
    reduce_scatter x2 -> x1, waiting for transfers between devices: 270 us -> 0.01 us  [body(): lax.psum_scatter(partial_value, 'head', scatter_dimension=1, tiled=True)]
    ppermute x0 -> x15, waiting for transfers between devices: none -> 184 us  [hop(): lax.ppermute(array, axis, [(i, i ^ flip) for i in range(lax.axis_size(axi...]
    all_gather x1 -> x0, waiting for transfers between devices: 175 us -> none  [body(): weights_all = lax.all_gather(projection, 'seq', axis=0, tiled=True)]
    dot_general x3 -> x24, matrix products: 77.2 us -> 133 us  [the longest x8 61.9 us: body(): jnp.einsum('td,kdc->ktc', feature_rows(owner, first, block.shape[1]), blo...]
    all_gather x1, waiting for transfers between devices: 110 us -> 55.9 us  [body(): features = lax.all_gather(inputs, 'head', axis=1, tiled=True)]
    all_gather x2 -> x0, blocking collectives: 20.6 us -> none  [prefix(): lax.all_gather(part.astype(kind), axis)]
    ppermute x0 -> x15, starting transfers between devices: none -> 18.8 us  [hop(): lax.ppermute(array, axis, [(i, i ^ flip) for i in range(lax.axis_size(axi...]
    unnamed x1 -> x0, blocking collectives: 8.9 us -> none
  transfers between devices with their start and end apart: 4 -> 17, of which waited for: 4 -> 7; matrix products, arithmetic and copies ran while one was open for 5% -> 22% of each run, Pallas kernels for 0% -> 0%
where the time goes in v1:
time: 538 us; the launch traced here: 528 us
  waiting for transfers between devices  241 us (45%)
  matrix products  160 us (30%)
  local copies, waits for them, and re-layouts  55.5 us (10%)
  other arithmetic  37.3 us (7%)
  starting transfers between devices  18.8 us (3%)
  between operations  15 us (3%)
    ppermute x15, waiting for transfers between devices, hop(): lax.ppermute(array, axis, [(i, i ^ flip) for i in range(lax.axis_size(axi...  184 us
    dot_general x8, matrix products, body(): jnp.einsum('td,kdc->ktc', feature_rows(owner, first, block.shape[1]), blo...  61.9 us
    all_gather x1, waiting for transfers between devices, body(): features = lax.all_gather(inputs, 'head', axis=1, tiled=True)  55.9 us
    dot_general x8, matrix products, body(): jnp.einsum('ktc,kdc->td', project_gradient, block, preferred_element_type...  41.1 us
    dot_general x8, matrix products, weight_partial(): jnp.einsum('td,ktc->kdc', feature_rows(owner, first, count), project_grad...  29.9 us
    ppermute x15, starting transfers between devices, hop(): lax.ppermute(array, axis, [(i, i ^ flip) for i in range(lax.axis_size(axi...  18.8 us
    unnamed x66, local copies, waits for them, and re-layouts  12 us
  transfers between devices with their start and end apart: 17, of which 7 were waited for; matrix products, arithmetic and copies ran while one was open for 22% of the time, Pallas kernels for 0%

profile of v1, /device:TPU:0, one launch (start us, length us, event | category | flops | bytes accessed | tf_op | source)
XLA Modules:
  0.0 528.0 jit_solution(1366227272367069007)
XLA Ops:
  8.0 5.3 %fusion.148 = (bf16[3,768,512]{2,1,0:T(8,128)(2,1)}, bf16[3,768,512]{2,1,0:T(8,128)(2,1)}) fusion(bf16[3,1536,512]{2,1,0:T(8,128)(2,1)} %bitcast.245), kind=kLoop, calls=%fused_computation.224 | loop fusion | bytes 9437184 | tf_op jit(solution)/shard_map/slice | solution.py:45
  18.5 4.8 reduce-window.6
  27.3 41.3 %collective-permute-done.1 = bf16[3,768,512]{2,1,0:T(8,128)(2,1)} collective-permute-done((bf16[3,768,512]{2,1,0:T(8,128)(2,1)}, bf16[3,768,512]{2,1,0:T(8,128)(2,1)}, u32[]{:S(2)}, u32[]{:S(2)}) %collective-permute-start.1) | collective-permute-done | bytes 2359328 | tf_op jit(solution)/shard_map/ppermute | solution.py:11
  73.2 55.9 %all-gather.2.cloned.1.call-done = bf16[1024,6144]{1,0:T(8,128)(2,1)} async-done(((bf16[1024,768]{1,0:T(8,128)(2,1)}), bf16[1024,6144]{1,0:T(8,128)(2,1)}) %all-gather.2.cloned.1.call-update) | async-done | bytes 12582928 | tf_op jit(solution)/shard_map/all_gather | solution.py:122
  129.1 7.5 %fusion.43 = f32[1024,3,512]{2,0,1:T(8,128)} fusion(bf16[3,768,512]{2,1,0:T(8,128)(2,1)} %collective-permute-done, bf16[1024,6144]{1,0:T(8,128)(2,1)} %all-gather.2.cloned.1.call-done, s32[]{:T(128)S(6)} %select_n.169), kind=kOutput, calls=%fused_computation.81 | convolution fusion | flops 2415919104 | bytes 10223620 | tf_op jit(solution)/shard_map/td,kdc->ktc/dot_general | solution.py:130
  136.6 7.5 %fusion.40 = f32[1024,3,512]{2,0,1:T(8,128)} fusion(bf16[3,768,512]{2,1,0:T(8,128)(2,1)} %collective-permute-done.1, bf16[1024,6144]{1,0:T(8,128)(2,1)} %all-gather.2.cloned.1.call-done, s32[]{:T(128)S(6)} %select_n.170), kind=kOutput, calls=%fused_computation.78 | convolution fusion | flops 2415919104 | bytes 10223620 | tf_op jit(solution)/shard_map/td,kdc->ktc/dot_general | solution.py:130
  144.2 4.6 fusion.47
  148.8 4.6 fusion.51
  153.4 17.0 %collective-permute-done.4 = bf16[3,768,512]{2,1,0:T(8,128)(2,1)} collective-permute-done((bf16[3,768,512]{2,1,0:T(8,128)(2,1)}, bf16[3,768,512]{2,1,0:T(8,128)(2,1)}, u32[]{:S(2)}, u32[]{:S(2)}) %collective-permute-start.4) | collective-permute-done | bytes 2359328 | tf_op jit(solution)/shard_map/ppermute | solution.py:11
  170.4 6.1 %fusion.31 = f32[1024,3,512]{2,0,1:T(8,128)} fusion(bf16[3,768,512]{2,1,0:T(8,128)(2,1)} %collective-permute-done.4, bf16[1024,6144]{1,0:T(8,128)(2,1)S(1)} %bitcast.256, s32[]{:T(128)S(6)} %select_n.173), kind=kOutput, calls=%fused_computation.69 | convolution fusion | flops 2415919104 | bytes 10223620 | tf_op jit(solution)/shard_map/td,kdc->ktc/dot_general | solution.py:130
  176.6 6.2 %fusion.34 = f32[1024,3,512]{2,0,1:T(8,128)} fusion(bf16[3,768,512]{2,1,0:T(8,128)(2,1)} %collective-permute-done.3, bf16[1024,6144]{1,0:T(8,128)(2,1)S(1)} %bitcast.256, s32[]{:T(128)S(6)} %select_n.172), kind=kOutput, calls=%fused_computation.72 | convolution fusion | flops 2415919104 | bytes 10223620 | tf_op jit(solution)/shard_map/td,kdc->ktc/dot_general | solution.py:130
  182.7 6.2 %fusion.37 = f32[1024,3,512]{2,0,1:T(8,128)} fusion(bf16[3,768,512]{2,1,0:T(8,128)(2,1)} %collective-permute-done.2, bf16[1024,6144]{1,0:T(8,128)(2,1)S(1)} %bitcast.256, s32[]{:T(128)S(6)} %select_n.171), kind=kOutput, calls=%fused_computation.75 | convolution fusion | flops 2415919104 | bytes 10223620 | tf_op jit(solution)/shard_map/td,kdc->ktc/dot_general | solution.py:130
  190.3 19.2 %add_bitcast_fusion = f32[3,1024,512]{2,1,0:T(8,128)} fusion(f32[1024,3,512]{2,0,1:T(8,128)} %fusion.31, f32[1024,3,512]{2,0,1:T(8,128)} %fusion.34, f32[1024,3,512]{2,0,1:T(8,128)} %fusion.37, f32[1024,3,512]{2,0,1:T(8,128)} %fusion.40, f32[1024,3,512]{2,0,1:T(8,128)} %fusion.43, f32[1024,3,512]{2,0,1:T(8,128)} %fusion.51, f32[1024,3,512]{2,0,1:T(8,128)} %fusion.47, ...), kind=kOutput, calls=%fused_computation.14 | convolution fusion | flops 2426929152 | bytes 54263812 | tf_op jit(solution)/shard_map/td,kdc->ktc/dot_general | solution.py:130
  227.8 7.3 %while.38 = (s32[]{:T(128)}, f32[4]{0:T(128)S(1)}, f32[4,128,128]{2,1,0:T(8,128)S(1)}, f32[4,4]{1,0:T(4,128)S(1)}, f32[4,4,128,128]{3,2,1,0:T(8,128)}, /*index=5...) while((s32[]{:T(128)}, f32[4]{0:T(128)S(1)}, ...), condition=%wide.region_5.6_spmd.clone, body=%wide.region_4.5_spmd.clone.sunk | while | flops 262155 | bytes 1311477 | solution.py:176
  235.3 4.3 convolution_bitcast_fusion
  240.7 7.4 %while.39 = (s32[]{:T(128)}, f32[4]{0:T(128)S(1)}, f32[4,128,128]{2,1,0:T(8,128)S(1)}, f32[4,4]{1,0:T(4,128)S(1)}, f32[4,4,128,128]{3,2,1,0:T(8,128)}, /*index=5...) while((s32[]{:T(128)}, f32[4]{0:T(128)S(1)}, ...), condition=%wide.region_7.8_spmd.clone, body=%wide.region_6.7_spmd.clone.sunk | while | flops 262156 | bytes 1310989 | solution.py:179
  256.2 5.5 %fusion.53 = f32[4,4,256,128]{3,2,1,0:T(8,128)} fusion(f32[4,4,256]{2,1,0:T(4,128)S(1)} %reduce_window_sum.30, pred[4,256,256]{1,2,0:T(8,128)(4,1)S(1)} %copy-done.19, bf16[4,256,4,128]{3,1,0,2:T(8,128)(2,1)S(1)} %multiply_convert_fusion.6, bf16[4,256,4,128]{3,2,1,0:T(4,128)(2,1)} %reshape.196, f32[4,256,4,128]{3,2,1,0:T(4,128)} %squeeze.48), kind=kOutput, calls=%fused_computation.91 | convolution fusion | flops 545259520 | bytes 6569984 | tf_op jit(solution)/shard_map/hbts,hbtf->hbsf/dot_general | solution.py:225
  292.3 5.4 %multiply_convert_fusion.2 = (bf16[1,1024,512]{2,1,0:T(8,128)(2,1)S(1)}, bf16[1,1024,512]{2,1,0:T(8,128)(2,1)}) fusion(f32[1,1024,512]{2,1,0:T(8,128)} %reshape.199, f32[3,1024,512]{2,1,0:T(8,128)} %add_bitcast_fusion, f32[1,1024,512]{2,1,0:T(8,128)S(1)} %copy-done.2), kind=kLoop, calls=%fused_computation.52 | loop fusion | flops 9961472 | bytes 10485760 | tf_op jit(solution)/shard_map/convert.6
  297.7 6.1 %broadcast_in_dim.91 = bf16[1024,6144]{1,0:T(8,128)(2,1)} broadcast(bf16[]{:T(256)} %constant.85.clone.1), dimensions={} | broadcast | bytes 12582914 | tf_op jit(solution)/shard_map/broadcast_in_dim | solution.py:246
  303.8 5.5 %fusion.17 = bf16[1024,6144]{1,0:T(8,128)(2,1)} fusion(bf16[1024,6144]{1,0:T(8,128)(2,1)} %broadcast_in_dim.91, s32[]{:T(128)S(6)} %select_n.167, bf16[3,1536,512]{2,1,0:T(8,128)(2,1)S(1)} %bitcast.252, bf16[1,1024,512]{2,1,0:T(8,128)(2,1)} %stack_reshape.4, bf16[1,1024,512]{2,1,0:T(8,128)(2,1)} %get-tuple-element.341, ...), kind=kOutput, calls=%fused_computation.57 | convolution fusion | flops 2419851264 | bytes 7077892 | tf_op jit(solution)/shard_map/ktc,kdc->td/dot_general | solution.py:248
  313.3 5.5 %fusion.19 = bf16[1024,6144]{1,0:T(8,128)(2,1)} fusion(bf16[1024,6144]{1,0:T(8,128)(2,1)} %fusion.18, s32[]{:T(128)S(6)} %select_n.169, bf16[3,768,512]{2,1,0:T(8,128)(2,1)} %collective-permute-done, bf16[1,1024,512]{2,1,0:T(8,128)(2,1)S(1)} %copy-done.15, bf16[1,1024,512]{2,1,0:T(8,128)(2,1)S(1)} %copy-done.12, ...), kind=kOutput, calls=%fused_computation.59 | convolution fusion | flops 2419851264 | bytes 7077892 | tf_op jit(solution)/shard_map/ktc,kdc->td/dot_general | solution.py:248
  318.8 5.5 %fusion.20 = bf16[1024,6144]{1,0:T(8,128)(2,1)} fusion(bf16[1024,6144]{1,0:T(8,128)(2,1)} %fusion.19, s32[]{:T(128)S(6)} %select_n.170, bf16[3,768,512]{2,1,0:T(8,128)(2,1)} %collective-permute-done.1, bf16[1,1024,512]{2,1,0:T(8,128)(2,1)S(1)} %copy-done.15, bf16[1,1024,512]{2,1,0:T(8,128)(2,1)S(1)} %copy-done.12, ...), kind=kOutput, calls=%fused_computation.60 | convolution fusion | flops 2419851264 | bytes 7077892 | tf_op jit(solution)/shard_map/ktc,kdc->td/dot_general | solution.py:248
  324.3 5.7 %fusion.21 = bf16[1024,6144]{1,0:T(8,128)(2,1)} fusion(bf16[1024,6144]{1,0:T(8,128)(2,1)} %fusion.20, s32[]{:T(128)S(6)} %select_n.171, bf16[3,768,512]{2,1,0:T(8,128)(2,1)} %collective-permute-done.2, bf16[1,1024,512]{2,1,0:T(8,128)(2,1)S(1)} %copy-done.15, bf16[1,1024,512]{2,1,0:T(8,128)(2,1)S(1)} %copy-done.12, ...), kind=kOutput, calls=%fused_computation.61 | convolution fusion | flops 2419851264 | bytes 7077892 | tf_op jit(solution)/shard_map/ktc,kdc->td/dot_general | solution.py:248
  330.0 5.5 %fusion.22 = bf16[1024,6144]{1,0:T(8,128)(2,1)} fusion(bf16[1024,6144]{1,0:T(8,128)(2,1)} %fusion.21, s32[]{:T(128)S(6)} %select_n.172, bf16[3,768,512]{2,1,0:T(8,128)(2,1)} %collective-permute-done.3, bf16[1,1024,512]{2,1,0:T(8,128)(2,1)S(1)} %copy-done.15, bf16[1,1024,512]{2,1,0:T(8,128)(2,1)S(1)} %copy-done.12, ...), kind=kOutput, calls=%fused_computation.62 | convolution fusion | flops 2419851264 | bytes 7077892 | tf_op jit(solution)/shard_map/ktc,kdc->td/dot_general | solution.py:248
  335.5 5.6 %fusion.23 = bf16[1024,6144]{1,0:T(8,128)(2,1)} fusion(bf16[1024,6144]{1,0:T(8,128)(2,1)} %fusion.22, s32[]{:T(128)S(6)} %select_n.173, bf16[3,768,512]{2,1,0:T(8,128)(2,1)} %collective-permute-done.4, bf16[1,1024,512]{2,1,0:T(8,128)(2,1)S(1)} %copy-done.15, bf16[1,1024,512]{2,1,0:T(8,128)(2,1)S(1)} %copy-done.12, ...), kind=kOutput, calls=%fused_computation.63 | convolution fusion | flops 2419851264 | bytes 7077892 | tf_op jit(solution)/shard_map/ktc,kdc->td/dot_general | solution.py:248
  346.8 4.6 convert_bitcast_fusion.2
  353.0 4.6 convert_bitcast_fusion.1
  368.2 37.5 %collective-permute-done.10 = bf16[3,768,512]{1,2,0:T(8,128)(2,1)S(1)} collective-permute-done((bf16[3,768,512]{1,2,0:T(8,128)(2,1)S(1)}, bf16[3,768,512]{1,2,0:T(8,128)(2,1)S(1)}, u32[]{:S(2)}, u32[]{:S(2)}) %collective-permute-start.10) | collective-permute-done | bytes 2359328 | tf_op jit(solution)/shard_map/ppermute | solution.py:11
  411.8 4.4 fusion.6
  423.7 32.5 %collective-permute-done.9 = bf16[3,768,512]{1,2,0:T(8,128)(2,1)S(1)} collective-permute-done((bf16[3,768,512]{1,2,0:T(8,128)(2,1)S(1)}, bf16[3,768,512]{1,2,0:T(8,128)(2,1)S(1)}, u32[]{:S(2)}, u32[]{:S(2)}) %collective-permute-start.9) | collective-permute-done | bytes 2359328 | tf_op jit(solution)/shard_map/ppermute | solution.py:11
  456.2 53.2 %collective-permute-done.11 = bf16[3,768,512]{1,2,0:T(8,128)(2,1)S(1)} collective-permute-done((bf16[3,768,512]{1,2,0:T(8,128)(2,1)S(1)}, bf16[3,768,512]{1,2,0:T(8,128)(2,1)S(1)}, u32[]{:S(2)}, u32[]{:S(2)}) %collective-permute-start.11) | collective-permute-done | bytes 2359328 | tf_op jit(solution)/shard_map/ppermute | solution.py:11
  514.1 6.6 %copy.172 = bf16[1536,3,512]{2,0,1:T(8,128)(2,1)} copy(bf16[1536,3,512]{0,2,1:T(8,128)(2,1)} %maximum_bitcast_fusion) | data formatting | bytes 9437184
  (210 shorter events, 128.8 us)
Async XLA Ops:
  7.2 121.9 %all-gather.2.cloned.1.call-start = ((), (), s32[]{:S(2)}) async-start(), calls=%async_computation.1 | async-start | bytes 14155776 | tf_op jit(solution)/shard_map/all_gather | solution.py:122
  7.9 512.8 %reduce-scatter.2.cloned.1.call-start = ((), (), s32[]{:S(2)}) async-start(), calls=%async_computation.2 | async-start | bytes 14155776 | tf_op jit(solution)/shard_map/reduce_scatter | solution.py:254
  7.9 10.4 %copy-start.21 = (s32[4]{0:T(128)S(1)}, s32[4]{0:T(128)}, u32[]{:S(2)}) copy-start(s32[4]{0:T(128)} %param.13) | copy-start | bytes 52
  8.0 10.5 %copy-start.20 = (f32[4,1024]{1,0:T(4,128)S(1)}, f32[4,1024]{1,0:T(4,128)}, u32[]{:S(2)}) copy-start(f32[4,1024]{1,0:T(4,128)} %param.12) | copy-start | bytes 49156
  8.0 15.8 %copy-start.14 = (bf16[1024,512]{1,0:T(8,128)(2,1)S(1)}, bf16[1024,512]{1,0:T(8,128)(2,1)}, u32[]{:S(2)}) copy-start(bf16[1024,512]{1,0:T(8,128)(2,1)} %param.11) | copy-start | bytes 3145732
  13.3 55.4 %collective-permute-start.1 = (bf16[3,768,512]{2,1,0:T(8,128)(2,1)}, bf16[3,768,512]{2,1,0:T(8,128)(2,1)}, u32[]{:S(2)}, u32[]{:S(2)}) collective-permute-start(bf16[3,768,512]{2,1,0:T(8,128)(2,1)} %get-tuple-element.345), channel_id=1, source_target_pairs={{0,16},{8,24},{16,0},{24,8},{1,17},{9,25},{17,1},{25,9},{2,18},{10... | collective-permute-start | bytes 7077896 | tf_op jit(solution)/shard_map/ppermute | solution.py:11
  16.3 55.4 %collective-permute-start = (bf16[3,768,512]{2,1,0:T(8,128)(2,1)}, bf16[3,768,512]{2,1,0:T(8,128)(2,1)}, u32[]{:S(2)}, u32[]{:S(2)}) collective-permute-start(bf16[3,768,512]{2,1,0:T(8,128)(2,1)} %get-tuple-element.344), channel_id=1, source_target_pairs={{0,8},{8,0},{16,24},{24,16},{1,9},{9,1},{17,25},{25,17},{2,10},{10... | collective-permute-start | bytes 7077896 | tf_op jit(solution)/shard_map/ppermute | solution.py:11
  17.8 158.8 %collective-permute-start.3 = (bf16[3,768,512]{2,1,0:T(8,128)(2,1)}, bf16[3,768,512]{2,1,0:T(8,128)(2,1)}, u32[]{:S(2)}, u32[]{:S(2)}) collective-permute-start(bf16[3,768,512]{2,1,0:T(8,128)(2,1)} %get-tuple-element.344), channel_id=1, source_target_pairs={{0,16},{8,24},{16,0},{24,8},{1,17},{9,25},{17,1},{25,9},{2,18},{10... | collective-permute-start | bytes 7077896 | tf_op jit(solution)/shard_map/ppermute | solution.py:11
  18.3 164.4 %collective-permute-start.2 = (bf16[3,768,512]{2,1,0:T(8,128)(2,1)}, bf16[3,768,512]{2,1,0:T(8,128)(2,1)}, u32[]{:S(2)}, u32[]{:S(2)}) collective-permute-start(bf16[3,768,512]{2,1,0:T(8,128)(2,1)} %get-tuple-element.345), channel_id=1, source_target_pairs={{0,8},{8,0},{16,24},{24,16},{1,9},{9,1},{17,25},{25,17},{2,10},{10... | collective-permute-start | bytes 7077896 | tf_op jit(solution)/shard_map/ppermute | solution.py:11
  68.7 101.8 %collective-permute-start.4 = (bf16[3,768,512]{2,1,0:T(8,128)(2,1)}, bf16[3,768,512]{2,1,0:T(8,128)(2,1)}, u32[]{:S(2)}, u32[]{:S(2)}) collective-permute-start(bf16[3,768,512]{2,1,0:T(8,128)(2,1)} %collective-permute-done.1), channel_id=1, source_target_pairs={{0,8},{8,0},{16,24},{24,16},{1,9},{9,1},{17,25},{25,17},{2,10},{10... | collective-permute-start | bytes 7077896 | tf_op jit(solution)/shard_map/ppermute | solution.py:11
  71.6 117.2 %collective-permute-start.5 = (bf16[3,768,512]{2,1,0:T(8,128)(2,1)}, bf16[3,768,512]{2,1,0:T(8,128)(2,1)S(1)}, u32[]{:S(2)}, u32[]{:S(2)}) collective-permute-start(bf16[3,768,512]{2,1,0:T(8,128)(2,1)} %collective-permute-done), channel_id=1, source_target_pairs={{0,16},{8,24},{16,0},{24,8},{1,17},{9,25},{17,1},{25,9},{2,18},{10... | collective-permute-start | bytes 7077896 | tf_op jit(solution)/shard_map/ppermute | solution.py:11
  129.1 15.1 %slice-start = ((s8[4718592]{0:T(1024)(128)(4,1)}), s8[4194304]{0:T(1024)(128)(4,1)S(1)}, s32[]{:S(2)}) async-start(s8[4718592]{0:T(1024)(128)(4,1)} %bitcast.246), calls=%async_computation.3 | async-start | bytes 8388608
  129.1 15.1 %slice-start.4 = ((s8[12582912]{0:T(1024)(128)(4,1)}), s8[4194304]{0:T(1024)(128)(4,1)S(1)}, s32[]{:S(2)}) async-start(s8[12582912]{0:T(1024)(128)(4,1)} %bitcast.255), calls=%async_computation.7 | async-start | bytes 8388608
  129.1 15.1 %slice-start.5 = ((s8[12582912]{0:T(1024)(128)(4,1)}), s8[4194304]{0:T(1024)(128)(4,1)S(1)}, s32[]{:S(2)}) async-start(s8[12582912]{0:T(1024)(128)(4,1)} %bitcast.255), calls=%async_computation.8 | async-start | bytes 8388608
  136.6 7.5 %slice-start.1 = ((s8[4718592]{0:T(1024)(128)(4,1)}), s8[524288]{0:T(1024)(128)(4,1)S(1)}, s32[]{:S(2)}) async-start(s8[4718592]{0:T(1024)(128)(4,1)} %bitcast.246), calls=%async_computation.4 | async-start | bytes 1048576
  136.6 7.5 %slice-start.6 = ((s8[12582912]{0:T(1024)(128)(4,1)}), s8[4194304]{0:T(1024)(128)(4,1)S(1)}, s32[]{:S(2)}) async-start(s8[12582912]{0:T(1024)(128)(4,1)} %bitcast.255), calls=%async_computation.9 | async-start | bytes 8388608
  248.9 7.3 %copy-start.19 = (pred[4,256,256]{1,2,0:T(8,128)(4,1)S(1)}, pred[4,256,256]{1,2,0:T(8,128)(4,1)}, u32[]{:S(2)}) copy-start(pred[4,256,256]{1,2,0:T(8,128)(4,1)} %compare_and_fusion) | copy-start | bytes 786436
  248.9 18.2 %collective-permute-start.6 = (bf16[9,128,128]{2,1,0:T(8,128)(2,1)}, bf16[9,128,128]{2,1,0:T(8,128)(2,1)S(1)}, u32[]{:S(2)}, u32[]{:S(2)}) collective-permute-start(bf16[9,128,128]{2,1,0:T(8,128)(2,1)} %pad_maximum_fusion.1), channel_id=1, source_target_pairs={{0,24},{8,16},{16,8},{24,0},{1,25},{9,17},{17,9},{25,1},{2,26},{10... | collective-permute-start | bytes 884744 | tf_op jit(solution)/shard_map/ppermute | solution.py:11
  250.3 16.8 %collective-permute-start.7 = (bf16[9,128,128]{2,1,0:T(8,128)(2,1)}, bf16[9,128,128]{2,1,0:T(8,128)(2,1)S(1)}, u32[]{:S(2)}, u32[]{:S(2)}) collective-permute-start(bf16[9,128,128]{2,1,0:T(8,128)(2,1)} %pad_maximum_fusion.1), channel_id=1, source_target_pairs={{0,16},{8,24},{16,0},{24,8},{1,17},{9,25},{17,1},{25,9},{2,18},{10... | collective-permute-start | bytes 884744 | tf_op jit(solution)/shard_map/ppermute | solution.py:11
  251.8 16.7 %collective-permute-start.8 = (bf16[9,128,128]{2,1,0:T(8,128)(2,1)}, bf16[9,128,128]{2,1,0:T(8,128)(2,1)}, u32[]{:S(2)}, u32[]{:S(2)}) collective-permute-start(bf16[9,128,128]{2,1,0:T(8,128)(2,1)} %pad_maximum_fusion.1), channel_id=1, source_target_pairs={{0,8},{8,0},{16,24},{24,16},{1,9},{9,1},{17,25},{25,17},{2,10},{10... | collective-permute-start | bytes 884744 | tf_op jit(solution)/shard_map/ppermute | solution.py:11
  292.3 11.5 %slice-start.2 = ((s8[4718592]{0:T(1024)(128)(4,1)}), s8[524288]{0:T(1024)(128)(4,1)S(1)}, s32[]{:S(2)}) async-start(s8[4718592]{0:T(1024)(128)(4,1)} %bitcast.250), calls=%async_computation.5 | async-start | bytes 1048576
  297.7 43.4 %copy-start.10 = (bf16[1,1024,512]{2,1,0:T(8,128)(2,1)}, bf16[1,1024,512]{2,1,0:T(8,128)(2,1)S(1)}, u32[]{:S(2)}) copy-start(bf16[1,1024,512]{2,1,0:T(8,128)(2,1)S(1)} %get-tuple-element.340) | copy-start | bytes 3145732
  297.7 6.1 %slice-start.3 = ((s8[4718592]{0:T(1024)(128)(4,1)}), s8[4194304]{0:T(1024)(128)(4,1)S(1)}, s32[]{:S(2)}) async-start(s8[4718592]{0:T(1024)(128)(4,1)} %bitcast.250), calls=%async_computation.6 | async-start | bytes 8388608
  346.8 11.7 %slice-start.7 = ((s8[12582912]{0:T(1024)(128)(4,1)}), s8[4194304]{0:T(1024)(128)(4,1)S(1)}, s32[]{:S(2)}) async-start(s8[12582912]{0:T(1024)(128)(4,1)} %bitcast.257), calls=%async_computation.10 | async-start | bytes 8388608
  346.8 11.7 %slice-start.8 = ((s8[12582912]{0:T(1024)(128)(4,1)}), s8[4194304]{0:T(1024)(128)(4,1)S(1)}, s32[]{:S(2)}) async-start(s8[12582912]{0:T(1024)(128)(4,1)} %bitcast.257), calls=%async_computation.11 | async-start | bytes 8388608
  351.4 7.2 %slice-start.9 = ((s8[12582912]{0:T(1024)(128)(4,1)}), s8[4194304]{0:T(1024)(128)(4,1)S(1)}, s32[]{:S(2)}) async-start(s8[12582912]{0:T(1024)(128)(4,1)} %bitcast.257), calls=%async_computation.12 | async-start | bytes 8388608
  351.4 54.3 %collective-permute-start.10 = (bf16[3,768,512]{1,2,0:T(8,128)(2,1)S(1)}, bf16[3,768,512]{1,2,0:T(8,128)(2,1)S(1)}, u32[]{:S(2)}, u32[]{:S(2)}) collective-permute-start(bf16[3,768,512]{1,2,0:T(8,128)(2,1)S(1)} %convert_bitcast_fusion.2), channel_id=1, source_target_pairs={{0,8},{8,0},{16,24},{24,16},{1,9},{9,1},{17,25},{25,17},{2,10},{10... | collective-permute-start | bytes 7077896 | tf_op jit(solution)/shard_map/ppermute | solution.py:11
  357.5 54.2 %collective-permute-start.12 = (bf16[3,768,512]{1,2,0:T(8,128)(2,1)S(1)}, bf16[3,768,512]{1,2,0:T(8,128)(2,1)S(1)}, u32[]{:S(2)}, u32[]{:S(2)}) collective-permute-start(bf16[3,768,512]{1,2,0:T(8,128)(2,1)S(1)} %convert_bitcast_fusion.1), channel_id=1, source_target_pairs={{0,16},{8,24},{16,0},{24,8},{1,17},{9,25},{17,1},{25,9},{2,18},{10... | collective-permute-start | bytes 7077896 | tf_op jit(solution)/shard_map/ppermute | solution.py:11
  361.6 94.6 %collective-permute-start.9 = (bf16[3,768,512]{1,2,0:T(8,128)(2,1)S(1)}, bf16[3,768,512]{1,2,0:T(8,128)(2,1)S(1)}, u32[]{:S(2)}, u32[]{:S(2)}) collective-permute-start(bf16[3,768,512]{1,2,0:T(8,128)(2,1)S(1)} %convert_bitcast_fusion.3), channel_id=1, source_target_pairs={{0,8},{8,0},{16,24},{24,16},{1,9},{9,1},{17,25},{25,17},{2,10},{10... | collective-permute-start | bytes 7077896 | tf_op jit(solution)/shard_map/ppermute | solution.py:11
  366.5 144.0 %collective-permute-start.14 = (bf16[3,768,512]{1,2,0:T(8,128)(2,1)}, bf16[3,768,512]{1,2,0:T(8,128)(2,1)S(1)}, u32[]{:S(2)}, u32[]{:S(2)}) collective-permute-start(bf16[3,768,512]{1,2,0:T(8,128)(2,1)} %convert_bitcast_fusion), channel_id=1, source_target_pairs={{0,16},{8,24},{16,0},{24,8},{1,17},{9,25},{17,1},{25,9},{2,18},{10... | collective-permute-start | bytes 7077896 | tf_op jit(solution)/shard_map/ppermute | solution.py:11
  408.8 100.7 %collective-permute-start.11 = (bf16[3,768,512]{1,2,0:T(8,128)(2,1)S(1)}, bf16[3,768,512]{1,2,0:T(8,128)(2,1)S(1)}, u32[]{:S(2)}, u32[]{:S(2)}) collective-permute-start(bf16[3,768,512]{1,2,0:T(8,128)(2,1)S(1)} %fusion.9), channel_id=1, source_target_pairs={{0,16},{8,24},{16,0},{24,8},{1,17},{9,25},{17,1},{25,9},{2,18},{10... | collective-permute-start | bytes 7077896 | tf_op jit(solution)/shard_map/ppermute | solution.py:11
  416.1 94.4 %collective-permute-start.13 = (bf16[3,768,512]{1,2,0:T(8,128)(2,1)}, bf16[3,768,512]{1,2,0:T(8,128)(2,1)S(1)}, u32[]{:S(2)}, u32[]{:S(2)}) collective-permute-start(bf16[3,768,512]{1,2,0:T(8,128)(2,1)} %fusion.6), channel_id=1, source_target_pairs={{0,8},{8,0},{16,24},{24,16},{1,9},{9,1},{17,25},{25,17},{2,10},{10... | collective-permute-start | bytes 7077896 | tf_op jit(solution)/shard_map/ppermute | solution.py:11
  (17 other events, 44.4 us)
Sparse Core Ops, SparseCore 0:
  9.6 119.4 all-gather.1
  345.1 129.5 reduce-scatter.1

commit v2 on v1

v2 whole, which is shorter than its diff:
```python
import jax
import jax.numpy as jnp
from jax import lax
from jax.experimental import pallas as pl
from jax.experimental.pallas import tpu as pltpu
from jax.sharding import PartitionSpec as P

HEAD_DIM = 128
BLOCK = 256


def hop(array, axis, flip):
    return lax.ppermute(array, axis, [(i, i ^ flip) for i in range(lax.axis_size(axis))])


def gather_states(packed, axis):
    length, place = (lax.axis_size(axis), lax.axis_index(axis))
    if length != 4:
        whole = lax.all_gather(packed, axis)
        return [whole[k] for k in range(length)], jnp.arange(length, dtype=jnp.int32)
    parts = [packed] + [hop(packed, axis, flip) for flip in range(1, length)]
    return parts, place ^ jnp.arange(length, dtype=jnp.int32)


def device_weights(device_decay, owners, axis):
    length, place = (lax.axis_size(axis), lax.axis_index(axis))
    decays = lax.all_gather(device_decay, axis)
    at, other = owners[:, None], jnp.arange(length, dtype=jnp.int32)[None]
    before = (other > at) & (other < place)
    after = (other < at) & (other > place)
    weights = []
    for between, counts in ((before, owners < place), (after, owners > place)):
        product = jnp.prod(jnp.where(between[:, :, None], decays[None], 1.0), axis=1)
        weights.append(jnp.where(counts[:, None], product, 0.0))
    return jnp.stack(weights)


def gather_rows(part, axis):
    length, place, rows = (lax.axis_size(axis), lax.axis_index(axis), part.shape[1])
    if length != 4:
        whole = lax.all_gather(part, axis, axis=1, tiled=True)
        return [(0, 0, whole)]
    half = rows // 2
    low, high = part[:, :half], part[:, half:]
    x_high = hop(high, axis, 1)
    y_low = hop(low, axis, 2)
    x_low = hop(low, axis, 1)
    y_high = hop(high, axis, 2)
    d_low = hop(y_low, axis, 1)
    d_high = hop(x_high, axis, 2)
    return [
        (place, 0, low),
        (place, half, high),
        (place ^ 1, half, x_high),
        (place ^ 2, 0, y_low),
        (place ^ 1, 0, x_low),
        (place ^ 2, half, y_high),
        (place ^ 3, 0, d_low),
        (place ^ 3, half, d_high),
    ]


def scatter_rows(partial, between, source, axis, rows):
    length, place = (lax.axis_size(axis), lax.axis_index(axis))
    if length != 4:
        whole = partial(source, 0, 0, rows * length)
        return between(source), lax.psum_scatter(whole, axis, scatter_dimension=1, tiled=True)
    half = rows // 2

    def add(*terms):
        return sum(term.astype(jnp.float32) for term in terms).astype(jnp.bfloat16)

    far_low, far_high = partial(source, place ^ 3, 0, half), partial(source, place ^ 3, half, half)
    source, far_low, far_high = lax.optimization_barrier((source, far_low, far_high))
    far_low, far_high = hop(far_low, axis, 1), hop(far_high, axis, 2)
    beside = between(source)
    source, beside = lax.optimization_barrier((source, beside))
    x_low = hop(partial(source, place ^ 1, 0, half), axis, 1)
    y_high = hop(partial(source, place ^ 2, half, half), axis, 2)
    x_high = hop(add(partial(source, place ^ 1, half, half), far_high), axis, 1)
    y_low = hop(add(partial(source, place ^ 2, 0, half), far_low), axis, 2)
    own_low, own_high = partial(source, place, 0, half), partial(source, place, half, half)
    whole = jnp.concatenate([add(own_low, x_low, y_low), add(own_high, x_high, y_high)], axis=1)
    return beside, whole


def block_factors(decay_sum, doc_index, doc_begin):
    inside = jnp.arange(doc_index.shape[-1], dtype=jnp.int32)
    causal = inside[:, None] >= inside[None, :]
    same_doc = (doc_index[:, :, None] == doc_index[:, None, :]) & causal[None]
    spread = jnp.minimum(decay_sum[..., :, None] - decay_sum[..., None, :], 0.0)
    pair_weight = jnp.where(same_doc[None], jnp.exp(spread), 0.0)
    to_end = jnp.where(
        (doc_index == doc_index[:, -1:])[None], jnp.exp(decay_sum[..., -1:] - decay_sum), 0.0
    )
    began_flag = doc_index == doc_index[:, :1] - doc_begin[:, :1]
    from_start = jnp.where(began_flag[None], jnp.exp(decay_sum), 0.0)
    return (pair_weight, to_end, from_start, from_start[..., -1])


def dot(left, right, contract):
    return lax.dot_general(
        left, right, ((contract[:1], contract[1:]), ((), ())), preferred_element_type=jnp.float32
    )


def projections(proj_ref, span):
    point_q, point_k = proj_ref[0, span], proj_ref[1, span]
    gate_q, gate_k = jax.nn.sigmoid(point_q), jax.nn.sigmoid(point_k)
    queries = (point_q * gate_q * HEAD_DIM ** (-0.5)).astype(jnp.bfloat16)
    keys = (point_k * gate_k).astype(jnp.bfloat16)
    values = proj_ref[2, span].astype(jnp.bfloat16)
    return (point_q, gate_q, queries), (point_k, gate_k, keys), values


def state_kernel(proj_ref, up_ref, start_ref, end_ref, key_ref, query_ref, total_ref):
    blocks = key_ref.shape[1]
    forward = jnp.zeros((HEAD_DIM, HEAD_DIM), jnp.float32)
    query_states, decays = [], []
    for b in range(blocks):
        span = pl.ds(b * BLOCK, BLOCK)
        (_, _, queries), (_, _, keys), values = projections(proj_ref, span)
        keys_weighted = (keys.astype(jnp.float32) * end_ref[0, span]).astype(jnp.bfloat16)
        queries_weighted = (queries.astype(jnp.float32) * start_ref[0, span]).astype(jnp.bfloat16)
        key_state = dot(keys_weighted, values, (0, 0))
        query_state = dot(queries_weighted, up_ref[span], (0, 0))
        key_ref[0, b] = key_state
        query_ref[0, b] = query_state
        decay = start_ref[0, pl.ds(b * BLOCK + BLOCK - 1, 1)]
        forward = decay * forward + key_state
        query_states.append(query_state)
        decays.append(decay)
    backward = jnp.zeros((HEAD_DIM, HEAD_DIM), jnp.float32)
    for b in reversed(range(blocks)):
        backward = decays[b] * backward + query_states[b]
    total_ref[0, 0] = forward.astype(jnp.bfloat16)
    total_ref[1, 0] = backward.astype(jnp.bfloat16)


def gradient_kernel(
    weight_ref, proj_ref, up_ref, start_ref, end_ref, pair_ref, key_ref, query_ref, *rest
):
    totals, out_ref = rest[:-1], rest[-1]
    blocks = key_ref.shape[1]
    head = pl.program_id(0)
    state = jnp.zeros((HEAD_DIM, HEAD_DIM), jnp.float32)
    reverse = jnp.zeros((HEAD_DIM, HEAD_DIM), jnp.float32)
    for k, total in enumerate(totals):
        state = state + weight_ref[0, k, head] * total[0, 0].astype(jnp.float32)
        reverse = reverse + weight_ref[1, k, head] * total[1, 0].astype(jnp.float32)
    decays = [start_ref[0, pl.ds(b * BLOCK + BLOCK - 1, 1)] for b in range(blocks)]
    after = [None] * blocks
    for b in reversed(range(blocks)):
        after[b] = reverse.astype(jnp.bfloat16)
        reverse = decays[b] * reverse + query_ref[0, b]
    for b in range(blocks):
        before = state.astype(jnp.bfloat16)
        state = decays[b] * state + key_ref[0, b]
        span = pl.ds(b * BLOCK, BLOCK)
        (point_q, gate_q, queries), (point_k, gate_k, keys), values = projections(proj_ref, span)
        upstream = up_ref[span]
        from_start, to_end, pair = start_ref[0, span], end_ref[0, span], pair_ref[0, b]
        query_key = (dot(queries, keys, (1, 1)) * pair).astype(jnp.bfloat16)
        value_score = (dot(upstream, values, (1, 1)) * pair).astype(jnp.bfloat16)
        query_gradient = dot(value_score, keys, (1, 0)) + from_start * dot(
            upstream, before, (1, 1)
        )
        key_gradient = dot(value_score, queries, (0, 0)) + to_end * dot(values, after[b], (1, 1))
        value_gradient = dot(query_key, upstream, (0, 0)) + to_end * dot(keys, after[b], (1, 0))
        slope_q = gate_q * (1.0 + point_q * (1.0 - gate_q)) * HEAD_DIM ** (-0.5)
        slope_k = gate_k * (1.0 + point_k * (1.0 - gate_k))
        out_ref[0, span] = (query_gradient * slope_q).astype(jnp.bfloat16)
        out_ref[1, span] = (key_gradient * slope_k).astype(jnp.bfloat16)
        out_ref[2, span] = value_gradient.astype(jnp.bfloat16)


def input_kernel(gradient_ref, weight_ref, out_ref):
    for first in range(0, out_ref.shape[0], BLOCK):
        span = pl.ds(first, BLOCK)
        total = dot(gradient_ref[0, span], weight_ref[0], (1, 1))
        for k in (1, 2):
            total = total + dot(gradient_ref[k, span], weight_ref[k], (1, 1))
        out_ref[span] = total.astype(jnp.bfloat16)


def body(inputs, projection, cotangent, log_decay, document_starts):
    tokens = inputs.shape[0]
    heads_here = log_decay.shape[0]
    local_cols = cotangent.shape[1]
    blocks = tokens // BLOCK
    features = lax.all_gather(inputs, "head", axis=1, tiled=True)
    rows = projection.shape[0]
    blocks_w = gather_rows(projection.transpose(1, 0, 2), "seq")

    def feature_rows(owner, first, count):
        return lax.dynamic_slice_in_dim(features, owner * rows + first, count, axis=1)

    projected = None
    weights_all = jnp.zeros((3, features.shape[1], local_cols), jnp.bfloat16)
    for owner, first, block in blocks_w:
        piece = jnp.einsum(
            "td,kdc->ktc",
            feature_rows(owner, first, block.shape[1]),
            block,
            preferred_element_type=jnp.float32,
        )
        projected = piece if projected is None else lax.optimization_barrier(projected) + piece
        weights_all = lax.dynamic_update_slice_in_dim(
            weights_all, block, owner * rows + first, axis=1
        )
    offset = lax.axis_index("seq") * tokens
    positions = offset + jnp.arange(tokens, dtype=jnp.int32)
    doc_index = (
        jnp.sum((document_starts[None, :] <= positions[:, None]).astype(jnp.int32), axis=1) - 1
    )
    doc_begin = jnp.any(document_starts[None, :] == positions[:, None], axis=1).astype(jnp.int32)
    decay_sum = jnp.cumsum(log_decay.reshape(heads_here, blocks, BLOCK), axis=-1)
    pair_weight, to_end, from_start, block_decay = block_factors(
        decay_sum, doc_index.reshape(blocks, BLOCK), doc_begin.reshape(blocks, BLOCK)
    )
    lanes = (heads_here, tokens, HEAD_DIM)
    to_end = jnp.broadcast_to(to_end.reshape(heads_here, tokens)[..., None], lanes)
    from_start = jnp.broadcast_to(from_start.reshape(heads_here, tokens)[..., None], lanes)
    device_decay = jnp.prod(block_decay, axis=1)

    proj_spec = pl.BlockSpec((3, tokens, HEAD_DIM), lambda h: (0, 0, h))
    up_spec = pl.BlockSpec((tokens, HEAD_DIM), lambda h: (0, h))
    lane_spec = pl.BlockSpec((1, tokens, HEAD_DIM), lambda h: (h, 0, 0))
    state_spec = pl.BlockSpec((1, blocks, HEAD_DIM, HEAD_DIM), lambda h: (h, 0, 0, 0))
    total_spec = pl.BlockSpec((2, 1, HEAD_DIM, HEAD_DIM), lambda h: (0, h, 0, 0))
    pair_spec = pl.BlockSpec((1, blocks, BLOCK, BLOCK), lambda h: (h, 0, 0, 0))
    states = jax.ShapeDtypeStruct((heads_here, blocks, HEAD_DIM, HEAD_DIM), jnp.float32)
    key_state, query_state, totals = pl.pallas_call(
        state_kernel,
        grid=(heads_here,),
        in_specs=[proj_spec, up_spec, lane_spec, lane_spec],
        out_specs=[state_spec, state_spec, total_spec],
        out_shape=[
            states,
            states,
            jax.ShapeDtypeStruct((2, heads_here, HEAD_DIM, HEAD_DIM), jnp.bfloat16),
        ],
    )(projected, cotangent, from_start, to_end)
    parts, owners = gather_states(totals, "seq")
    weights = device_weights(device_decay, owners, "seq")
    project_gradient = pl.pallas_call(
        gradient_kernel,
        grid=(heads_here,),
        in_specs=[pl.BlockSpec(memory_space=pltpu.SMEM)]
        + [proj_spec, up_spec, lane_spec, lane_spec, pair_spec, state_spec, state_spec]
        + [total_spec] * len(parts),
        out_specs=proj_spec,
        out_shape=jax.ShapeDtypeStruct(projected.shape, jnp.bfloat16),
    )(weights, projected, cotangent, from_start, to_end, pair_weight, key_state, query_state, *parts)

    def weight_partial(gradient, owner, first, count):
        return jnp.einsum(
            "td,ktc->kdc",
            feature_rows(owner, first, count),
            gradient,
            preferred_element_type=jnp.float32,
        ).astype(jnp.bfloat16)

    def input_partial(gradient):
        columns = features.shape[1]
        tile = columns // 8
        return pl.pallas_call(
            input_kernel,
            grid=(columns // tile,),
            in_specs=[
                pl.BlockSpec(gradient.shape, lambda i: (0, 0, 0)),
                pl.BlockSpec((3, tile, local_cols), lambda i: (0, i, 0)),
            ],
            out_specs=pl.BlockSpec((tokens, tile), lambda i: (0, i)),
            out_shape=jax.ShapeDtypeStruct((tokens, columns), jnp.bfloat16),
            cost_estimate=pl.CostEstimate(flops=1, bytes_accessed=1, transcendentals=0),
            compiler_params=pltpu.CompilerParams(vmem_limit_bytes=40 << 20),
        )(gradient, weights_all)

    partial_value, weight_gradient = scatter_rows(
        weight_partial, input_partial, project_gradient, "seq", rows
    )
    input_gradient = lax.psum_scatter(partial_value, "head", scatter_dimension=1, tiled=True)
    weight_gradient = weight_gradient.transpose(1, 0, 2)
    return (input_gradient, weight_gradient)


def solution(mesh):
    placed = (P("seq", "head"), P("seq", None, "head"), P("seq", "head"), P("head", "seq"), P())
    return jax.shard_map(
        body,
        mesh=mesh,
        in_specs=placed,
        out_specs=(P("seq", "head"), P("seq", None, "head")),
        check_vma=False,
    )
```

time: 538 us -> 444 us (0.83); the launches traced: 528 us -> 440 us
  waiting for transfers between devices: 241 us -> 124 us
  blocking collectives: 0 us -> 97.8 us
  matrix products: 160 us -> 76.6 us
  Pallas kernels: 0 us -> 41.9 us
  other arithmetic: 37.3 us -> 24.1 us
  local copies, waits for them, and re-layouts: 55.5 us -> 43.7 us
    unnamed x0 -> x1, blocking collectives: none -> 97.8 us
    ppermute x15, waiting for transfers between devices: 184 us -> 124 us  [hop(): lax.ppermute(array, axis, [(i, i ^ flip) for i in range(lax.axis_size(axi...]
    dot_general x25 -> x8, matrix products: 98.5 us -> 38.2 us  [weight_partial(): jnp.einsum('td,ktc->kdc', feature_rows(owner, first, count), gradient, pr...]
    all_gather x1, waiting for transfers between devices: 55.9 us -> 0.01 us  [body(): features = lax.all_gather(inputs, 'head', axis=1, tiled=True)]
    pallas_call x0 -> x3, Pallas kernels: none -> 41.9 us  [the longest x1 24.2 us: input_partial(): pl.pallas_call(input_kernel, grid=(columns // tile,), in_specs=[pl.BlockS...]
    dot_general x8, matrix products: 61.9 us -> 38.4 us  [body(): jnp.einsum('td,kdc->ktc', feature_rows(owner, first, block.shape[1]), blo...]
    dynamic_update_slice x8, local copies, waits for them, and re-layouts: 0.32 us -> 23.3 us  [body(): lax.dynamic_update_slice_in_dim(weights_all, block, owner * rows + first,...]
    slice x5 -> x3, local copies, waits for them, and re-layouts: 12.2 us -> 0.29 us  [the longest x1 5.33 us: gather_rows(): low, high = (part[:, :half], part[:, half:])]
  transfers between devices with their start and end apart: 17 -> 17, of which waited for: 7 -> 5; matrix products, arithmetic and copies ran while one was open for 22% -> 27% of each run, Pallas kernels for 0% -> 0%
where the time goes in v2:
time: 444 us; the launch traced here: 440 us
  waiting for transfers between devices  124 us (28%)
  blocking collectives  97.8 us (22%)
  matrix products  76.6 us (17%)
  local copies, waits for them, and re-layouts  43.7 us (10%)
  Pallas kernels  41.9 us (9%)
  other arithmetic  24.1 us (5%)
  starting transfers between devices  16.3 us (4%)
  between operations  15.2 us (3%)
    ppermute x15, waiting for transfers between devices, hop(): lax.ppermute(array, axis, [(i, i ^ flip) for i in range(lax.axis_size(axi...  124 us
    unnamed x1, blocking collectives  97.8 us
    dot_general x8, matrix products, body(): jnp.einsum('td,kdc->ktc', feature_rows(owner, first, block.shape[1]), blo...  38.4 us
    dot_general x8, matrix products, weight_partial(): jnp.einsum('td,ktc->kdc', feature_rows(owner, first, count), gradient, pr...  38.2 us
    pallas_call x1, Pallas kernels, input_partial(): pl.pallas_call(input_kernel, grid=(columns // tile,), in_specs=[pl.BlockS...  24.2 us
    dynamic_update_slice x8, local copies, waits for them, and re-layouts, body(): lax.dynamic_update_slice_in_dim(weights_all, block, owner * rows + first,...  23.3 us
    ppermute x15, starting transfers between devices, hop(): lax.ppermute(array, axis, [(i, i ^ flip) for i in range(lax.axis_size(axi...  16.2 us
    pallas_call x1, Pallas kernels, body(): pl.pallas_call(gradient_kernel, grid=(heads_here,), in_specs=[pl.BlockSpe...  11 us
  transfers between devices with their start and end apart: 17, of which 5 were waited for; matrix products, arithmetic and copies ran while one was open for 27% of the time, Pallas kernels for 0%

profile of v2, /device:TPU:0, one launch (start us, length us, event | category | flops | bytes accessed | tf_op | source)
XLA Modules:
  0.0 439.9 jit_solution(5217926151959072915)
XLA Ops:
  8.0 7.3 %broadcast_in_dim.127 = bf16[3,6144,512]{2,1,0:T(8,128)(2,1)} broadcast(bf16[]{:T(256)} %constant.40.clone.1), dimensions={} | broadcast | bytes 18874370 | tf_op jit(solution)/shard_map/broadcast_in_dim | solution.py:199
  16.8 3.7 constant_dynamic-update-slice_fusion.6
  26.2 4.8 %reduce-window.6 = f32[4,4,2,128]{3,2,1,0:T(2,128)S(1)} reduce-window(f32[4,4,2,128]{3,2,1,0:T(2,128)S(1)} %reshape.295, f32[]{:T(128)} %constant.12.clone.1), window={size=1x1x1x128 pad=0_0x0_0x0_0x127_0}, to_apply=%region_2.0 | reduce-window | flops 520192 | bytes 32772 | tf_op jit(solution)/shard_map/reduce-window
  33.6 97.8 %all-reduce = f32[16]{0:T(128)S(1)} all-reduce(f32[16]{0:T(128)S(1)} %dynamic-update-slice), channel_id=2, replica_groups=mesh['seq'=4,'head'=8] {'seq'}, use_global_device_ids=true, to_apply=%add | all-reduce | flops 16 | bytes 128
  144.6 3.3 constant_dynamic-update-slice_fusion.2
  148.0 4.7 %convolution_bitcast_fusion = f32[3,1024,512]{2,1,0:T(8,128)S(1)} fusion(bf16[1024,6144]{1,0:T(8,128)(2,1)} %all-gather.3.cloned.1.call-done, s32[]{:T(128)S(6)} %select_n.94, bf16[3,1536,512]{2,1,0:T(8,128)(2,1)} %bitcast.115), kind=kOutput, calls=%fused_computation.19 | convolution fusion | flops 2415919104 | bytes 10223620 | tf_op jit(solution)/shard_map/td,kdc->ktc/dot_general | solution.py:201
  152.7 4.8 %bitcast_add_fusion.6 = f32[3,1024,512]{2,1,0:T(8,128)S(1)} fusion(f32[3,1024,512]{2,1,0:T(8,128)S(1)} %convolution_bitcast_fusion, bf16[1024,6144]{1,0:T(8,128)(2,1)} %all-gather.3.cloned.1.call-done, s32[]{:T(128)S(6)} %select_n.95, bf16[3,1536,512]{2,1,0:T(8,128)(2,1)} %bitcast.116), kind=kOutput, calls=%fused_computation.6 | convolution fusion | flops 2417491968 | bytes 16515076 | tf_op jit(solution)/shard_map/td,kdc->ktc/dot_general | solution.py:201
  157.5 4.8 %bitcast_add_fusion.5 = f32[3,1024,512]{2,1,0:T(8,128)S(1)} fusion(f32[3,1024,512]{2,1,0:T(8,128)S(1)} %bitcast_add_fusion.6, bf16[3,768,512]{2,1,0:T(8,128)(2,1)} %collective-permute-done, bf16[1024,6144]{1,0:T(8,128)(2,1)} %all-gather.3.cloned.1.call-done, s32[]{:T(128)S(6)} %select_n.96), kind=kOutput, calls=%fused_computation.5 | convolution fusion | flops 2417491968 | bytes 16515076 | tf_op jit(solution)/shard_map/td,kdc->ktc/dot_general | solution.py:201
  162.3 4.8 %fusion.19 = f32[1024,3,512]{2,0,1:T(8,128)S(1)} fusion(bf16[3,768,512]{2,1,0:T(8,128)(2,1)} %collective-permute-done.1, bf16[1024,6144]{1,0:T(8,128)(2,1)} %all-gather.3.cloned.1.call-done, s32[]{:T(128)S(6)} %select_n.97), kind=kOutput, calls=%fused_computation.37 | convolution fusion | flops 2415919104 | bytes 10223620 | tf_op jit(solution)/shard_map/td,kdc->ktc/dot_general | solution.py:201
  168.7 4.8 %fusion.15 = f32[1024,3,512]{2,0,1:T(8,128)S(1)} fusion(bf16[3,768,512]{2,1,0:T(8,128)(2,1)} %copy-done.1, bf16[1024,6144]{1,0:T(8,128)(2,1)} %all-gather.3.cloned.1.call-done, s32[]{:T(128)S(6)} %select_n.98), kind=kOutput, calls=%fused_computation.33 | convolution fusion | flops 2415919104 | bytes 10223620 | tf_op jit(solution)/shard_map/td,kdc->ktc/dot_general | solution.py:201
  175.0 5.0 %fusion.12 = f32[1024,3,512]{2,0,1:T(8,128)S(1)} fusion(bf16[3,768,512]{2,1,0:T(8,128)(2,1)} %collective-permute-done.3, bf16[1024,6144]{1,0:T(8,128)(2,1)} %all-gather.3.cloned.1.call-done, s32[]{:T(128)S(6)} %select_n.99), kind=kOutput, calls=%fused_computation.30 | convolution fusion | flops 2415919104 | bytes 10223620 | tf_op jit(solution)/shard_map/td,kdc->ktc/dot_general | solution.py:201
  181.5 5.4 %collective-permute-done.4 = bf16[3,768,512]{2,1,0:T(8,128)(2,1)} collective-permute-done((bf16[3,768,512]{2,1,0:T(8,128)(2,1)}, bf16[3,768,512]{2,1,0:T(8,128)(2,1)}, u32[]{:S(2)}, u32[]{:S(2)}) %collective-permute-start.4) | collective-permute-done | bytes 2359328 | tf_op jit(solution)/shard_map/ppermute | solution.py:13
  186.9 4.8 %bitcast_add_fusion.1 = f32[3,1024,512]{2,1,0:T(8,128)S(1)} fusion(f32[3,1024,512]{2,1,0:T(8,128)S(1)} %bitcast_add_fusion.2, bf16[3,768,512]{2,1,0:T(8,128)(2,1)} %collective-permute-done.4, bf16[1024,6144]{1,0:T(8,128)(2,1)} %all-gather.3.cloned.1.call-done, s32[]{:T(128)S(6)} %select_n.100), kind=kOutput, calls=%fused_computation.1 | convolution fusion | flops 2417491968 | bytes 16515076 | tf_op jit(solution)/shard_map/td,kdc->ktc/dot_general | solution.py:201
  191.7 4.8 %fusion.7 = f32[1024,3,512]{2,0,1:T(8,128)S(1)} fusion(bf16[3,768,512]{2,1,0:T(8,128)(2,1)} %collective-permute-done.5, bf16[1024,6144]{1,0:T(8,128)(2,1)} %all-gather.3.cloned.1.call-done, s32[]{:T(128)S(6)} %select_n.101), kind=kOutput, calls=%fused_computation.25 | convolution fusion | flops 2415919104 | bytes 10223620 | tf_op jit(solution)/shard_map/td,kdc->ktc/dot_general | solution.py:201
  196.5 4.2 bitcast_add_fusion.proj_ref
  204.6 6.7 %shard_map.68 = (f32[4,4,128,128]{3,2,1,0:T(8,128)}, f32[4,4,128,128]{3,2,1,0:T(8,128)}, bf16[2,4,128,128]{3,2,1,0:T(8,128)(2,1)}) custom-call(f32[3,1024,512]{2,1,0:T(8,128)} %bitcast_add_fusion.proj_ref, bf16[1024,512]{1,0:T(8,128)(2,1)} %up_ref.3, f32[4,1024,128]{2,1,0:T(8,128)} %broadcast_in_dim.123.start_ref, f32[4,1024,128]{2,1,0:T(8,128)} %broadcast_in_dim.125.end_ref), custom_call_target="tpu_custom_call" | custom-call | tf_op jit(solution)/shard_map/pallas_call | solution.py:233
  214.8 3.3 constant_dynamic-update-slice_fusion.1
  218.0 3.3 constant_dynamic-update-slice_fusion.weight_ref
  223.5 11.0 %shard_map.69.gradient_ref = bf16[3,1024,512]{2,1,0:T(8,128)(2,1)} custom-call(f32[2,4,4]{2,1,0:T(4,128)} %pad_maximum_fusion.weight_ref, f32[3,1024,512]{2,1,0:T(8,128)} %bitcast_add_fusion.proj_ref, bf16[1024,512]{1,0:T(8,128)(2,1)} %up_ref.3, f32[4,1024,128]{2,1,0:T(8,128)} %broadcast_in_dim.123.start_ref, f32[4,1024,128]{2,1,0:T(8,128)} %broadcast_in_dim.125.end_ref, ...), custom_call_target="tpu_custom_call" | custom-call | tf_op jit(solution)/shard_map/pallas_call | solution.py:246
  234.5 6.6 %convert_bitcast_fusion.2 = bf16[3,768,512]{1,2,0:T(8,128)(2,1)} fusion(bf16[3,1024,512]{2,1,0:T(8,128)(2,1)} %shard_map.69.gradient_ref, bf16[1024,6144]{1,0:T(8,128)(2,1)} %all-gather.3.cloned.1.call-done, s32[]{:T(128)S(6)} %select_n.101), kind=kOutput, calls=%fused_computation.22 | convolution fusion | flops 2417098752 | bytes 7077892 | tf_op jit(solution)/shard_map/td,ktc->kdc/dot_general | solution.py:257
  241.1 5.3 %convert_bitcast_fusion.3 = bf16[3,768,512]{1,2,0:T(8,128)(2,1)} fusion(bf16[3,1024,512]{2,1,0:T(8,128)(2,1)S(1)} %copy-done, bf16[1024,6144]{1,0:T(8,128)(2,1)} %all-gather.3.cloned.1.call-done, s32[]{:T(128)S(6)} %select_n.100), kind=kOutput, calls=%fused_computation.23 | convolution fusion | flops 2417098752 | bytes 7077892 | tf_op jit(solution)/shard_map/td,ktc->kdc/dot_general | solution.py:257
  246.4 24.2 %shard_map.70 = bf16[1024,6144]{1,0:T(8,128)(2,1)} custom-call(bf16[3,1024,512]{2,1,0:T(8,128)(2,1)S(1)} %copy-done, bf16[3,6144,512]{2,1,0:T(8,128)(2,1)} %constant_dynamic-update-slice_fusion.weight_ref), custom_call_target="tpu_custom_call" | custom-call | flops 1 | bytes 1 | tf_op jit(solution)/shard_map/pallas_call | solution.py:267
  272.8 4.3 convert_bitcast_fusion.1
  278.2 4.4 convert_bitcast_fusion
  283.8 4.3 fusion.17
  288.1 37.0 %collective-permute-done.10 = bf16[3,768,512]{1,2,0:T(8,128)(2,1)S(1)} collective-permute-done((bf16[3,768,512]{1,2,0:T(8,128)(2,1)}, bf16[3,768,512]{1,2,0:T(8,128)(2,1)S(1)}, u32[]{:S(2)}, u32[]{:S(2)}) %collective-permute-start.10) | collective-permute-done | bytes 2359328 | tf_op jit(solution)/shard_map/ppermute | solution.py:13
  326.7 4.5 %fusion.21 = bf16[3,512,768]{2,1,0:T(8,128)(2,1)S(1)} fusion(bf16[3,1024,512]{2,1,0:T(8,128)(2,1)S(1)} %copy-done, bf16[1024,6144]{1,0:T(8,128)(2,1)} %all-gather.3.cloned.1.call-done, s32[]{:T(128)S(6)} %select_n.96), kind=kOutput, calls=%fused_computation.39 | convolution fusion | flops 2415919104 | bytes 7077892 | tf_op jit(solution)/shard_map/td,ktc->kdc/dot_general | solution.py:257
  333.0 4.3 fusion.27
  337.4 4.4 fusion.24
  341.7 33.9 %collective-permute-done.9 = bf16[3,768,512]{1,2,0:T(8,128)(2,1)S(1)} collective-permute-done((bf16[3,768,512]{1,2,0:T(8,128)(2,1)S(1)}, bf16[3,768,512]{1,2,0:T(8,128)(2,1)S(1)}, u32[]{:S(2)}, u32[]{:S(2)}) %collective-permute-start.9) | collective-permute-done | bytes 2359328 | tf_op jit(solution)/shard_map/ppermute | solution.py:13
  375.7 46.0 %collective-permute-done.11 = bf16[3,768,512]{1,2,0:T(8,128)(2,1)S(1)} collective-permute-done((bf16[3,768,512]{1,2,0:T(8,128)(2,1)S(1)}, bf16[3,768,512]{1,2,0:T(8,128)(2,1)S(1)}, u32[]{:S(2)}, u32[]{:S(2)}) %collective-permute-start.11) | collective-permute-done | bytes 2359328 | tf_op jit(solution)/shard_map/ppermute | solution.py:13
  426.3 6.6 %copy.57 = bf16[1536,3,512]{2,0,1:T(8,128)(2,1)} copy(bf16[1536,3,512]{0,2,1:T(8,128)(2,1)} %maximum_bitcast_fusion) | data formatting | bytes 9437184
  (108 shorter events, 49.6 us)
Async XLA Ops:
  7.2 140.8 %all-gather.3.cloned.1.call-start = ((), (), s32[]{:S(2)}) async-start(), calls=%async_computation.1 | async-start | bytes 14155776 | tf_op jit(solution)/shard_map/all_gather | solution.py:191
  7.2 8.1 %slice-start = ((s8[4718592]{0:T(1024)(128)(4,1)}), s8[524288]{0:T(1024)(128)(4,1)S(1)}, s32[]{:S(2)}) async-start(s8[4718592]{0:T(1024)(128)(4,1)} %bitcast.117), calls=%async_computation.3 | async-start | bytes 1048576
  7.9 425.0 %reduce-scatter.2.cloned.1.call-start = ((), (), s32[]{:S(2)}) async-start(), calls=%async_computation.2 | async-start | bytes 14155776 | tf_op jit(solution)/shard_map/reduce_scatter | solution.py:283
  8.0 7.3 %slice-start.1 = ((s8[4718592]{0:T(1024)(128)(4,1)}), s8[4194304]{0:T(1024)(128)(4,1)S(1)}, s32[]{:S(2)}) async-start(s8[4718592]{0:T(1024)(128)(4,1)} %bitcast.117), calls=%async_computation.4 | async-start | bytes 8388608
  16.8 8.8 %copy-start.6 = (s32[4]{0:T(128)S(1)}, s32[4]{0:T(128)}, u32[]{:S(2)}) copy-start(s32[4]{0:T(128)} %param.9) | copy-start | bytes 52
  16.8 9.4 %copy-start.5 = (f32[4,1024]{1,0:T(4,128)S(1)}, f32[4,1024]{1,0:T(4,128)}, u32[]{:S(2)}) copy-start(f32[4,1024]{1,0:T(4,128)} %param.8) | copy-start | bytes 49156
  16.8 15.2 %copy-start.7 = (u32[32]{0:T(128)S(1)}, u32[32]{0:T(128)}, u32[]{:S(2)}) copy-start(u32[32]{0:T(128)} %constant.44) | copy-start | bytes 388
  20.6 114.8 %collective-permute-start.1 = (bf16[3,768,512]{2,1,0:T(8,128)(2,1)}, bf16[3,768,512]{2,1,0:T(8,128)(2,1)}, u32[]{:S(2)}, u32[]{:S(2)}) collective-permute-start(bf16[3,768,512]{2,1,0:T(8,128)(2,1)} %get-tuple-element.32), channel_id=1, source_target_pairs={{0,16},{8,24},{16,0},{24,8},{1,17},{9,25},{17,1},{25,9},{2,18},{10... | collective-permute-start | bytes 7077896 | tf_op jit(solution)/shard_map/ppermute | solution.py:13
  23.6 119.3 %collective-permute-start.2 = (bf16[3,768,512]{2,1,0:T(8,128)(2,1)}, bf16[3,768,512]{2,1,0:T(8,128)(2,1)S(1)}, u32[]{:S(2)}, u32[]{:S(2)}) collective-permute-start(bf16[3,768,512]{2,1,0:T(8,128)(2,1)} %get-tuple-element.32), channel_id=1, source_target_pairs={{0,8},{8,0},{16,24},{24,16},{1,9},{9,1},{17,25},{25,17},{2,10},{10... | collective-permute-start | bytes 7077896 | tf_op jit(solution)/shard_map/ppermute | solution.py:13
  25.1 110.4 %collective-permute-start = (bf16[3,768,512]{2,1,0:T(8,128)(2,1)}, bf16[3,768,512]{2,1,0:T(8,128)(2,1)}, u32[]{:S(2)}, u32[]{:S(2)}) collective-permute-start(bf16[3,768,512]{2,1,0:T(8,128)(2,1)} %get-tuple-element.31), channel_id=1, source_target_pairs={{0,8},{8,0},{16,24},{24,16},{1,9},{9,1},{17,25},{25,17},{2,10},{10... | collective-permute-start | bytes 7077896 | tf_op jit(solution)/shard_map/ppermute | solution.py:13
  25.6 119.0 %collective-permute-start.3 = (bf16[3,768,512]{2,1,0:T(8,128)(2,1)}, bf16[3,768,512]{2,1,0:T(8,128)(2,1)}, u32[]{:S(2)}, u32[]{:S(2)}) collective-permute-start(bf16[3,768,512]{2,1,0:T(8,128)(2,1)} %get-tuple-element.31), channel_id=1, source_target_pairs={{0,16},{8,24},{16,0},{24,8},{1,17},{9,25},{17,1},{25,9},{2,18},{10... | collective-permute-start | bytes 7077896 | tf_op jit(solution)/shard_map/ppermute | solution.py:13
  135.4 51.5 %collective-permute-start.4 = (bf16[3,768,512]{2,1,0:T(8,128)(2,1)}, bf16[3,768,512]{2,1,0:T(8,128)(2,1)}, u32[]{:S(2)}, u32[]{:S(2)}) collective-permute-start(bf16[3,768,512]{2,1,0:T(8,128)(2,1)} %collective-permute-done.1), channel_id=1, source_target_pairs={{0,8},{8,0},{16,24},{24,16},{1,9},{9,1},{17,25},{25,17},{2,10},{10... | collective-permute-start | bytes 7077896 | tf_op jit(solution)/shard_map/ppermute | solution.py:13
  135.5 56.2 %collective-permute-start.5 = (bf16[3,768,512]{2,1,0:T(8,128)(2,1)}, bf16[3,768,512]{2,1,0:T(8,128)(2,1)}, u32[]{:S(2)}, u32[]{:S(2)}) collective-permute-start(bf16[3,768,512]{2,1,0:T(8,128)(2,1)} %collective-permute-done), channel_id=1, source_target_pairs={{0,16},{8,24},{16,0},{24,8},{1,17},{9,25},{17,1},{25,9},{2,18},{10... | collective-permute-start | bytes 7077896 | tf_op jit(solution)/shard_map/ppermute | solution.py:13
  143.0 5.0 %copy-start.1 = (bf16[3,768,512]{2,1,0:T(8,128)(2,1)}, bf16[3,768,512]{2,1,0:T(8,128)(2,1)S(1)}, u32[]{:S(2)}) copy-start(bf16[3,768,512]{2,1,0:T(8,128)(2,1)S(1)} %collective-permute-done.2) | copy-start | bytes 7077892
  211.3 10.0 %collective-permute-start.6 = (bf16[2,4,128,128]{3,2,1,0:T(8,128)(2,1)}, bf16[2,4,128,128]{3,2,1,0:T(8,128)(2,1)S(1)}, u32[]{:S(2)}, u32[]{:S(2)}) collective-permute-start(bf16[2,4,128,128]{3,2,1,0:T(8,128)(2,1)} %get-tuple-element.12.rest_0_), channel_id=1, source_target_pairs={{0,8},{8,0},{16,24},{24,16},{1,9},{9,1},{17,25},{25,17},{2,10},{10... | collective-permute-start | bytes 786440 | tf_op jit(solution)/shard_map/ppermute | solution.py:13
  211.6 11.1 %collective-permute-start.7 = (bf16[2,4,128,128]{3,2,1,0:T(8,128)(2,1)}, bf16[2,4,128,128]{3,2,1,0:T(8,128)(2,1)S(1)}, u32[]{:S(2)}, u32[]{:S(2)}) collective-permute-start(bf16[2,4,128,128]{3,2,1,0:T(8,128)(2,1)} %get-tuple-element.12.rest_0_), channel_id=1, source_target_pairs={{0,16},{8,24},{16,0},{24,8},{1,17},{9,25},{17,1},{25,9},{2,18},{10... | collective-permute-start | bytes 786440 | tf_op jit(solution)/shard_map/ppermute | solution.py:13
  212.6 10.1 %collective-permute-start.8 = (bf16[2,4,128,128]{3,2,1,0:T(8,128)(2,1)}, bf16[2,4,128,128]{3,2,1,0:T(8,128)(2,1)S(1)}, u32[]{:S(2)}, u32[]{:S(2)}) collective-permute-start(bf16[2,4,128,128]{3,2,1,0:T(8,128)(2,1)} %get-tuple-element.12.rest_0_), channel_id=1, source_target_pairs={{0,24},{8,16},{16,8},{24,0},{1,25},{9,17},{17,9},{25,1},{2,26},{10... | collective-permute-start | bytes 786440 | tf_op jit(solution)/shard_map/ppermute | solution.py:13
  221.3 1.3 copy-start.2
  222.6 0.7 copy-start.3
  222.6 0.8 copy-start.4
  234.5 6.6 %copy-start = (bf16[3,1024,512]{2,1,0:T(8,128)(2,1)S(1)}, bf16[3,1024,512]{2,1,0:T(8,128)(2,1)}, u32[]{:S(2)}) copy-start(bf16[3,1024,512]{2,1,0:T(8,128)(2,1)} %shard_map.69.gradient_ref) | copy-start | bytes 9437188
  270.6 54.5 %collective-permute-start.10 = (bf16[3,768,512]{1,2,0:T(8,128)(2,1)}, bf16[3,768,512]{1,2,0:T(8,128)(2,1)S(1)}, u32[]{:S(2)}, u32[]{:S(2)}) collective-permute-start(bf16[3,768,512]{1,2,0:T(8,128)(2,1)} %convert_bitcast_fusion.3), channel_id=1, source_target_pairs={{0,8},{8,0},{16,24},{24,16},{1,9},{9,1},{17,25},{25,17},{2,10},{10... | collective-permute-start | bytes 7077896 | tf_op jit(solution)/shard_map/ppermute | solution.py:13
  272.2 59.1 %collective-permute-start.12 = (bf16[3,768,512]{1,2,0:T(8,128)(2,1)}, bf16[3,768,512]{1,2,0:T(8,128)(2,1)S(1)}, u32[]{:S(2)}, u32[]{:S(2)}) collective-permute-start(bf16[3,768,512]{1,2,0:T(8,128)(2,1)} %convert_bitcast_fusion.2), channel_id=1, source_target_pairs={{0,16},{8,24},{16,0},{24,8},{1,17},{9,25},{17,1},{25,9},{2,18},{10... | collective-permute-start | bytes 7077896 | tf_op jit(solution)/shard_map/ppermute | solution.py:13
  277.1 98.5 %collective-permute-start.9 = (bf16[3,768,512]{1,2,0:T(8,128)(2,1)S(1)}, bf16[3,768,512]{1,2,0:T(8,128)(2,1)S(1)}, u32[]{:S(2)}, u32[]{:S(2)}) collective-permute-start(bf16[3,768,512]{1,2,0:T(8,128)(2,1)S(1)} %convert_bitcast_fusion.1), channel_id=1, source_target_pairs={{0,8},{8,0},{16,24},{24,16},{1,9},{9,1},{17,25},{25,17},{2,10},{10... | collective-permute-start | bytes 7077896 | tf_op jit(solution)/shard_map/ppermute | solution.py:13
  282.5 140.1 %collective-permute-start.14 = (bf16[3,768,512]{1,2,0:T(8,128)(2,1)S(1)}, bf16[3,768,512]{1,2,0:T(8,128)(2,1)S(1)}, u32[]{:S(2)}, u32[]{:S(2)}) collective-permute-start(bf16[3,768,512]{1,2,0:T(8,128)(2,1)S(1)} %convert_bitcast_fusion), channel_id=1, source_target_pairs={{0,16},{8,24},{16,0},{24,8},{1,17},{9,25},{17,1},{25,9},{2,18},{10... | collective-permute-start | bytes 7077896 | tf_op jit(solution)/shard_map/ppermute | solution.py:13
  325.6 96.0 %collective-permute-start.11 = (bf16[3,768,512]{1,2,0:T(8,128)(2,1)S(1)}, bf16[3,768,512]{1,2,0:T(8,128)(2,1)S(1)}, u32[]{:S(2)}, u32[]{:S(2)}) collective-permute-start(bf16[3,768,512]{1,2,0:T(8,128)(2,1)S(1)} %fusion.3), channel_id=1, source_target_pairs={{0,16},{8,24},{16,0},{24,8},{1,17},{9,25},{17,1},{25,9},{2,18},{10... | collective-permute-start | bytes 7077896 | tf_op jit(solution)/shard_map/ppermute | solution.py:13
  331.9 90.8 %collective-permute-start.13 = (bf16[3,768,512]{1,2,0:T(8,128)(2,1)S(1)}, bf16[3,768,512]{1,2,0:T(8,128)(2,1)S(1)}, u32[]{:S(2)}, u32[]{:S(2)}) collective-permute-start(bf16[3,768,512]{1,2,0:T(8,128)(2,1)S(1)} %fusion), channel_id=1, source_target_pairs={{0,8},{8,0},{16,24},{24,16},{1,9},{9,1},{17,25},{25,17},{2,10},{10... | collective-permute-start | bytes 7077896 | tf_op jit(solution)/shard_map/ppermute | solution.py:13
Sparse Core Ops, SparseCore 0:
  9.6 119.4 all-gather.2
  270.8 129.1 reduce-scatter.1

commit v3 on v2

--- a/solution.py
+++ b/solution.py
@@ -2,6 +2,7 @@
 import jax.numpy as jnp
 from jax import lax
 from jax.experimental import pallas as pl
+from jax.experimental.layout import Layout, with_layout_constraint
 from jax.experimental.pallas import tpu as pltpu
 from jax.sharding import PartitionSpec as P
 
@@ -24,7 +25,14 @@
 
 def device_weights(device_decay, owners, axis):
     length, place = (lax.axis_size(axis), lax.axis_index(axis))
-    decays = lax.all_gather(device_decay, axis)
+    if length == 4:
+        slab = jnp.broadcast_to(device_decay[:, None], (device_decay.shape[0], HEAD_DIM))
+        hops = [slab] + [hop(slab, axis, flip) for flip in range(1, length)]
+        arrived = jnp.stack([part[:, 0] for part in hops])
+        mine = owners[None, :] == jnp.arange(length, dtype=jnp.int32)[:, None]
+        decays = jnp.sum(jnp.where(mine[:, :, None], arrived[None], 0.0), axis=1)
+    else:
+        decays = lax.all_gather(device_decay, axis)
     at, other = owners[:, None], jnp.arange(length, dtype=jnp.int32)[None]
     before = (other > at) & (other < place)
     after = (other < at) & (other > place)
@@ -64,7 +72,7 @@
     length, place = (lax.axis_size(axis), lax.axis_index(axis))
     if length != 4:
         whole = partial(source, 0, 0, rows * length)
-        return between(source), lax.psum_scatter(whole, axis, scatter_dimension=1, tiled=True)
+        return [between(source, 0, 1)], lax.psum_scatter(whole, axis, scatter_dimension=1, tiled=True)
     half = rows // 2
 
     def add(*terms):
@@ -73,15 +81,16 @@
     far_low, far_high = partial(source, place ^ 3, 0, half), partial(source, place ^ 3, half, half)
     source, far_low, far_high = lax.optimization_barrier((source, far_low, far_high))
     far_low, far_high = hop(far_low, axis, 1), hop(far_high, axis, 2)
-    beside = between(source)
+    beside = between(source, 0, 1)
     source, beside = lax.optimization_barrier((source, beside))
-    x_low = hop(partial(source, place ^ 1, 0, half), axis, 1)
-    y_high = hop(partial(source, place ^ 2, half, half), axis, 2)
+    x_low, y_high = partial(source, place ^ 1, 0, half), partial(source, place ^ 2, half, half)
+    source, x_low, y_high = lax.optimization_barrier((source, x_low, y_high))
+    x_low, y_high = hop(x_low, axis, 1), hop(y_high, axis, 2)
     x_high = hop(add(partial(source, place ^ 1, half, half), far_high), axis, 1)
     y_low = hop(add(partial(source, place ^ 2, 0, half), far_low), axis, 2)
     own_low, own_high = partial(source, place, 0, half), partial(source, place, half, half)
     whole = jnp.concatenate([add(own_low, x_low, y_low), add(own_high, x_high, y_high)], axis=1)
-    return beside, whole
+    return [beside], whole
 
 
 def block_factors(decay_sum, doc_index, doc_begin):
@@ -195,9 +204,40 @@
     def feature_rows(owner, first, count):
         return lax.dynamic_slice_in_dim(features, owner * rows + first, count, axis=1)
 
+    offset = lax.axis_index("seq") * tokens
+    positions = offset + jnp.arange(tokens, dtype=jnp.int32)
+    doc_index = (
+        jnp.sum((document_starts[None, :] <= positions[:, None]).astype(jnp.int32), axis=1) - 1
+    )
+    doc_begin = jnp.any(document_starts[None, :] == positions[:, None], axis=1).astype(jnp.int32)
+    decay_sum = jnp.cumsum(log_decay.reshape(heads_here, blocks, BLOCK), axis=-1)
+    pair_weight, to_end, from_start, block_decay = block_factors(
+        decay_sum, doc_index.reshape(blocks, BLOCK), doc_begin.reshape(blocks, BLOCK)
+    )
+    lanes = (heads_here, tokens, HEAD_DIM)
+    to_end = jnp.broadcast_to(to_end.reshape(heads_here, tokens)[..., None], lanes)
+    from_start = jnp.broadcast_to(from_start.reshape(heads_here, tokens)[..., None], lanes)
+    device_decay = jnp.prod(block_decay, axis=1)
+
+    zero = jnp.zeros((), jnp.bfloat16)
+    if len(blocks_w) > 2:
+        owner, first, block = blocks_w[2]
+        zero, block = lax.optimization_barrier((zero, block))
+        blocks_w[2] = (owner, first, block)
+    weights_all = jnp.broadcast_to(zero, (3, features.shape[1], local_cols))
+
+    def place_rows(whole, some):
+        for owner, first, block in some:
+            whole = lax.dynamic_update_slice_in_dim(whole, block, owner * rows + first, axis=1)
+        return whole
+
+    early, late = blocks_w[:6], blocks_w[6:]
+    weights_all = place_rows(weights_all, early)
+    features, weights_all, from_start, to_end, pair_weight = lax.optimization_barrier(
+        (features, weights_all, from_start, to_end, pair_weight)
+    )
     projected = None
-    weights_all = jnp.zeros((3, features.shape[1], local_cols), jnp.bfloat16)
-    for owner, first, block in blocks_w:
+    for k, (owner, first, block) in enumerate(blocks_w):
         piece = jnp.einsum(
             "td,kdc->ktc",
             feature_rows(owner, first, block.shape[1]),
@@ -205,23 +245,9 @@
             preferred_element_type=jnp.float32,
         )
         projected = piece if projected is None else lax.optimization_barrier(projected) + piece
-        weights_all = lax.dynamic_update_slice_in_dim(
-            weights_all, block, owner * rows + first, axis=1
-        )
-    offset = lax.axis_index("seq") * tokens
-    positions = offset + jnp.arange(tokens, dtype=jnp.int32)
-    doc_index = (
-        jnp.sum((document_starts[None, :] <= positions[:, None]).astype(jnp.int32), axis=1) - 1
-    )
-    doc_begin = jnp.any(document_starts[None, :] == positions[:, None], axis=1).astype(jnp.int32)
-    decay_sum = jnp.cumsum(log_decay.reshape(heads_here, blocks, BLOCK), axis=-1)
-    pair_weight, to_end, from_start, block_decay = block_factors(
-        decay_sum, doc_index.reshape(blocks, BLOCK), doc_begin.reshape(blocks, BLOCK)
-    )
-    lanes = (heads_here, tokens, HEAD_DIM)
-    to_end = jnp.broadcast_to(to_end.reshape(heads_here, tokens)[..., None], lanes)
-    from_start = jnp.broadcast_to(from_start.reshape(heads_here, tokens)[..., None], lanes)
-    device_decay = jnp.prod(block_decay, axis=1)
+        if k == min(5, len(blocks_w) - 1):
+            projected, device_decay = lax.optimization_barrier((projected, device_decay))
+    weights_all = place_rows(weights_all, late)
 
     proj_spec = pl.BlockSpec((3, tokens, HEAD_DIM), lambda h: (0, 0, h))
     up_spec = pl.BlockSpec((tokens, HEAD_DIM), lambda h: (0, h))
@@ -254,33 +280,36 @@
     )(weights, projected, cotangent, from_start, to_end, pair_weight, key_state, query_state, *parts)
 
     def weight_partial(gradient, owner, first, count):
-        return jnp.einsum(
+        term = jnp.einsum(
             "td,ktc->kdc",
             feature_rows(owner, first, count),
             gradient,
             preferred_element_type=jnp.float32,
         ).astype(jnp.bfloat16)
-
-    def input_partial(gradient):
+        return with_layout_constraint(term, Layout(major_to_minor=(0, 1, 2)))
+
+    def input_partial(gradient, part, of):
         columns = features.shape[1]
-        tile = columns // 8
+        tile, count = columns // 8, tokens // of
         return pl.pallas_call(
             input_kernel,
             grid=(columns // tile,),
             in_specs=[
-                pl.BlockSpec(gradient.shape, lambda i: (0, 0, 0)),
+                pl.BlockSpec((3, count, local_cols), lambda i: (0, part, 0)),
                 pl.BlockSpec((3, tile, local_cols), lambda i: (0, i, 0)),
             ],
-            out_specs=pl.BlockSpec((tokens, tile), lambda i: (0, i)),
-            out_shape=jax.ShapeDtypeStruct((tokens, columns), jnp.bfloat16),
+            out_specs=pl.BlockSpec((count, tile), lambda i: (0, i)),
+            out_shape=jax.ShapeDtypeStruct((count, columns), jnp.bfloat16),
             cost_estimate=pl.CostEstimate(flops=1, bytes_accessed=1, transcendentals=0),
             compiler_params=pltpu.CompilerParams(vmem_limit_bytes=40 << 20),
         )(gradient, weights_all)
 
-    partial_value, weight_gradient = scatter_rows(
+    input_partials, weight_gradient = scatter_rows(
         weight_partial, input_partial, project_gradient, "seq", rows
     )
-    input_gradient = lax.psum_scatter(partial_value, "head", scatter_dimension=1, tiled=True)
+    input_gradient = lax.psum_scatter(
+        input_partials[0], "head", scatter_dimension=1, tiled=True
+    )
     weight_gradient = weight_gradient.transpose(1, 0, 2)
     return (input_gradient, weight_gradient)
 

time: 444 us -> 430 us (0.968)
  blocking collectives: 97.8 us -> 0 us
  waiting for transfers between devices: 124 us -> 209 us
  starting transfers between devices: 16.3 us -> 22.9 us
  local copies, waits for them, and re-layouts: 43.7 us -> 37.8 us
    unnamed x1 -> x0, blocking collectives: 97.8 us -> none
    ppermute x15 -> x18, waiting for transfers between devices: 124 us -> 208 us  [hop(): lax.ppermute(array, axis, [(i, i ^ flip) for i in range(lax.axis_size(axi...]
    unnamed x27, local copies, waits for them, and re-layouts: 8.5 us -> 0.94 us
    ppermute x15 -> x18, starting transfers between devices: 16.2 us -> 22.8 us  [hop(): lax.ppermute(array, axis, [(i, i ^ flip) for i in range(lax.axis_size(axi...]
    slice x2 -> x4, local copies, waits for them, and re-layouts: 0.21 us -> 6.11 us  [the longest x2 5.89 us: gather_rows(): low, high = (part[:, :half], part[:, half:])]
    dynamic_update_slice x8 -> x7, local copies, waits for them, and re-layouts: 23.3 us -> 19.8 us  [place_rows(): lax.dynamic_update_slice_in_dim(whole, block, owner * rows + first, axis=1)]
  transfers between devices with their start and end apart: 17 -> 20, of which waited for: 5 -> 9; matrix products, arithmetic and copies ran while one was open for 27% -> 30% of each run, Pallas kernels for 0% -> 2%
where the time goes in v3:
time: 430 us; the launch traced here: 427 us
  waiting for transfers between devices  209 us (49%)
  matrix products  76.5 us (18%)
  Pallas kernels  41.8 us (10%)
  local copies, waits for them, and re-layouts  37.8 us (9%)
  other arithmetic  24.4 us (6%)
  starting transfers between devices  22.9 us (5%)
  between operations  14.6 us (3%)
    ppermute x18, waiting for transfers between devices, hop(): lax.ppermute(array, axis, [(i, i ^ flip) for i in range(lax.axis_size(axi...  208 us
    dot_general x8, matrix products, weight_partial(): jnp.einsum('td,ktc->kdc', feature_rows(owner, first, count), gradient, pr...  38.8 us
    dot_general x8, matrix products, body(): jnp.einsum('td,kdc->ktc', feature_rows(owner, first, block.shape[1]), blo...  37.7 us
    pallas_call x1, Pallas kernels, input_partial(): pl.pallas_call(input_kernel, grid=(columns // tile,), in_specs=[pl.BlockS...  24.1 us
    ppermute x18, starting transfers between devices, hop(): lax.ppermute(array, axis, [(i, i ^ flip) for i in range(lax.axis_size(axi...  22.8 us
    dynamic_update_slice x7, local copies, waits for them, and re-layouts, place_rows(): lax.dynamic_update_slice_in_dim(whole, block, owner * rows + first, axis=1)  19.8 us
    pallas_call x1, Pallas kernels, body(): pl.pallas_call(gradient_kernel, grid=(heads_here,), in_specs=[pl.BlockSpe...  11 us
    add x4, other arithmetic, body(): lax.optimization_barrier(projected) + piece  8.9 us
  transfers between devices with their start and end apart: 20, of which 9 were waited for; matrix products, arithmetic and copies ran while one was open for 30% of the time, Pallas kernels for 2%

profile of v3, /device:TPU:0, one launch (start us, length us, event | category | flops | bytes accessed | tf_op | source)
XLA Modules:
  0.0 426.6 jit_solution(17599466933661812466)
XLA Ops:
  15.9 4.8 %reduce-window.6 = f32[4,4,2,128]{3,2,1,0:T(2,128)S(1)} reduce-window(f32[4,4,2,128]{3,2,1,0:T(2,128)S(1)} %reshape.321, f32[]{:T(128)} %constant.38.clone.1), window={size=1x1x1x128 pad=0_0x0_0x0_0x127_0}, to_apply=%region_2.0 | reduce-window | flops 520192 | bytes 32772 | tf_op jit(solution)/shard_map/reduce-window
  21.4 44.3 %collective-permute-done = bf16[3,768,512]{2,1,0:T(8,128)(2,1)} collective-permute-done((bf16[3,768,512]{2,1,0:T(8,128)(2,1)}, bf16[3,768,512]{2,1,0:T(8,128)(2,1)}, u32[]{:S(2)}, u32[]{:S(2)}) %collective-permute-start) | collective-permute-done | bytes 2359328 | tf_op jit(solution)/shard_map/ppermute | solution.py:14
  65.7 6.7 %broadcast_in_dim.138 = bf16[3,6144,512]{2,1,0:T(8,128)(2,1)} broadcast(bf16[]{:T(256)} %constant.16.clone.1), dimensions={} | broadcast | bytes 18874370 | tf_op jit(solution)/shard_map/broadcast_in_dim | solution.py:227
  84.4 3.3 constant_dynamic-update-slice_fusion.5
  87.7 43.4 %collective-permute-done.1 = bf16[3,768,512]{2,1,0:T(8,128)(2,1)} collective-permute-done((bf16[3,768,512]{2,1,0:T(8,128)(2,1)}, bf16[3,768,512]{2,1,0:T(8,128)(2,1)}, u32[]{:S(2)}, u32[]{:S(2)}) %collective-permute-start.1) | collective-permute-done | bytes 2359328 | tf_op jit(solution)/shard_map/ppermute | solution.py:14
  145.0 4.8 %convolution_bitcast_fusion = f32[3,1024,512]{2,1,0:T(8,128)S(1)} fusion(bf16[1024,6144]{1,0:T(8,128)(2,1)} %all-gather.2.cloned.1.call-done, s32[]{:T(128)S(6)} %select_n.92, bf16[3,1536,512]{2,1,0:T(8,128)(2,1)} %bitcast.118), kind=kOutput, calls=%fused_computation.13 | convolution fusion | flops 2415919104 | bytes 10223620 | tf_op jit(solution)/shard_map/td,kdc->ktc/dot_general | solution.py:241
  149.9 4.0 bitcast_add_fusion.6
  153.9 4.8 %bitcast_add_fusion.5 = f32[3,1024,512]{2,1,0:T(8,128)S(1)} fusion(f32[3,1024,512]{2,1,0:T(8,128)S(1)} %bitcast_add_fusion.6, bf16[3,768,512]{2,1,0:T(8,128)(2,1)} %collective-permute-done, bf16[1024,6144]{1,0:T(8,128)(2,1)} %all-gather.2.cloned.1.call-done, s32[]{:T(128)S(6)} %select_n.94), kind=kOutput, calls=%fused_computation.5 | convolution fusion | flops 2417491968 | bytes 16515076 | tf_op jit(solution)/shard_map/td,kdc->ktc/dot_general | solution.py:241
  158.7 4.8 %fusion.13 = f32[1024,3,512]{2,0,1:T(8,128)S(1)} fusion(bf16[3,768,512]{2,1,0:T(8,128)(2,1)} %collective-permute-done.1, bf16[1024,6144]{1,0:T(8,128)(2,1)} %all-gather.2.cloned.1.call-done, s32[]{:T(128)S(6)} %select_n.95), kind=kOutput, calls=%fused_computation.31 | convolution fusion | flops 2415919104 | bytes 10223620 | tf_op jit(solution)/shard_map/td,kdc->ktc/dot_general | solution.py:241
  165.1 4.8 %fusion.9 = f32[1024,3,512]{2,0,1:T(8,128)S(1)} fusion(bf16[3,768,512]{2,1,0:T(8,128)(2,1)} %collective-permute-done.2, bf16[1024,6144]{1,0:T(8,128)(2,1)} %all-gather.2.cloned.1.call-done, s32[]{:T(128)S(6)} %select_n.96), kind=kOutput, calls=%fused_computation.27 | convolution fusion | flops 2415919104 | bytes 10223620 | tf_op jit(solution)/shard_map/td,kdc->ktc/dot_general | solution.py:241
  171.4 5.0 %fusion.6 = f32[1024,3,512]{2,0,1:T(8,128)S(1)} fusion(bf16[3,768,512]{2,1,0:T(8,128)(2,1)} %copy-done.1, bf16[1024,6144]{1,0:T(8,128)(2,1)} %all-gather.2.cloned.1.call-done, s32[]{:T(128)S(6)} %select_n.97), kind=kOutput, calls=%fused_computation.24 | convolution fusion | flops 2415919104 | bytes 10223620 | tf_op jit(solution)/shard_map/td,kdc->ktc/dot_general | solution.py:241
  182.8 4.8 %bitcast_add_fusion.1 = f32[3,1024,512]{2,1,0:T(8,128)S(1)} fusion(f32[3,1024,512]{2,1,0:T(8,128)S(1)} %bitcast_add_fusion.2, bf16[3,768,512]{2,1,0:T(8,128)(2,1)} %collective-permute-done.7, bf16[1024,6144]{1,0:T(8,128)(2,1)} %all-gather.2.cloned.1.call-done, s32[]{:T(128)S(6)} %select_n.107), kind=kOutput, calls=%fused_computation.1 | convolution fusion | flops 2417491968 | bytes 16515076 | tf_op jit(solution)/shard_map/td,kdc->ktc/dot_general | solution.py:241
  187.6 4.8 %fusion.1 = f32[1024,3,512]{2,0,1:T(8,128)S(1)} fusion(bf16[3,768,512]{2,1,0:T(8,128)(2,1)} %collective-permute-done.8, bf16[1024,6144]{1,0:T(8,128)(2,1)} %all-gather.2.cloned.1.call-done, s32[]{:T(128)S(6)} %select_n.108), kind=kOutput, calls=%fused_computation.19 | convolution fusion | flops 2415919104 | bytes 10223620 | tf_op jit(solution)/shard_map/td,kdc->ktc/dot_general | solution.py:241
  192.4 4.2 bitcast_add_fusion.proj_ref
  196.6 6.7 %shard_map.68 = (f32[4,4,128,128]{3,2,1,0:T(8,128)}, f32[4,4,128,128]{3,2,1,0:T(8,128)}, bf16[2,4,128,128]{3,2,1,0:T(8,128)(2,1)}) custom-call(f32[3,1024,512]{2,1,0:T(8,128)} %bitcast_add_fusion.proj_ref, bf16[1024,512]{1,0:T(8,128)(2,1)} %up_ref.3, f32[4,1024,128]{2,1,0:T(8,128)} %broadcast_in_dim.141.start_ref, f32[4,1024,128]{2,1,0:T(8,128)} %broadcast_in_dim.143.end_ref), custom_call_target="tpu_custom_call" | custom-call | tf_op jit(solution)/shard_map/pallas_call | solution.py:259
  205.9 3.3 constant_dynamic-update-slice_fusion.1
  209.2 3.4 constant_dynamic-update-slice_fusion.weight_ref
  214.3 5.5 %collective-permute-done.11.rest_3_ = bf16[2,4,128,128]{3,2,1,0:T(8,128)(2,1)S(1)} collective-permute-done((bf16[2,4,128,128]{3,2,1,0:T(8,128)(2,1)S(1)}, bf16[2,4,128,128]{3,2,1,0:T(8,128)(2,1)S(1)}, u32[]{:S(2)}, u32[]{:S(2)}) %collective-permute-start.11) | collective-permute-done | bytes 262176 | tf_op jit(solution)/shard_map/ppermute | solution.py:14
  220.5 11.0 %shard_map.69.gradient_ref = bf16[3,1024,512]{2,1,0:T(8,128)(2,1)} custom-call(f32[2,4,4]{2,1,0:T(4,128)} %pad_maximum_fusion.weight_ref, f32[3,1024,512]{2,1,0:T(8,128)} %bitcast_add_fusion.proj_ref, bf16[1024,512]{1,0:T(8,128)(2,1)} %up_ref.3, f32[4,1024,128]{2,1,0:T(8,128)} %broadcast_in_dim.141.start_ref, f32[4,1024,128]{2,1,0:T(8,128)} %broadcast_in_dim.143.end_ref, ...), custom_call_target="tpu_custom_call" | custom-call | tf_op jit(solution)/shard_map/pallas_call | solution.py:272
  231.6 6.6 %convert_bitcast_fusion.3 = bf16[3,768,512]{2,1,0:T(8,128)(2,1)} fusion(bf16[3,1024,512]{2,1,0:T(8,128)(2,1)} %shard_map.69.gradient_ref, bf16[1024,6144]{1,0:T(8,128)(2,1)} %all-gather.2.cloned.1.call-done, s32[]{:T(128)S(6)} %select_n.107), kind=kOutput, calls=%fused_computation.17 | convolution fusion | flops 2417098752 | bytes 7077892 | tf_op jit(solution)/shard_map/td,ktc->kdc/dot_general | solution.py:283
  238.2 5.3 %convert_bitcast_fusion.2 = bf16[3,768,512]{2,1,0:T(8,128)(2,1)} fusion(bf16[3,1024,512]{2,1,0:T(8,128)(2,1)S(1)} %copy-done, bf16[1024,6144]{1,0:T(8,128)(2,1)} %all-gather.2.cloned.1.call-done, s32[]{:T(128)S(6)} %select_n.108), kind=kOutput, calls=%fused_computation.16 | convolution fusion | flops 2417098752 | bytes 7077892 | tf_op jit(solution)/shard_map/td,ktc->kdc/dot_general | solution.py:283
  243.5 24.1 %shard_map.70 = bf16[1024,6144]{1,0:T(8,128)(2,1)} custom-call(bf16[3,1024,512]{2,1,0:T(8,128)(2,1)S(1)} %copy-done, bf16[3,6144,512]{2,1,0:T(8,128)(2,1)} %constant_dynamic-update-slice_fusion.weight_ref), custom_call_target="tpu_custom_call" | custom-call | flops 1 | bytes 1 | tf_op jit(solution)/shard_map/pallas_call | solution.py:294
  268.9 4.4 %convert_bitcast_fusion.1 = bf16[3,768,512]{2,1,0:T(8,128)(2,1)S(1)} fusion(bf16[3,1024,512]{2,1,0:T(8,128)(2,1)S(1)} %copy-done, bf16[1024,6144]{1,0:T(8,128)(2,1)} %all-gather.2.cloned.1.call-done, s32[]{:T(128)S(6)} %select_n.96), kind=kOutput, calls=%fused_computation.15 | convolution fusion | flops 2417098752 | bytes 7077892 | tf_op jit(solution)/shard_map/td,ktc->kdc/dot_general | solution.py:283
  273.3 4.7 %convert_bitcast_fusion = bf16[3,768,512]{2,1,0:T(8,128)(2,1)S(1)} fusion(bf16[3,1024,512]{2,1,0:T(8,128)(2,1)S(1)} %copy-done, bf16[1024,6144]{1,0:T(8,128)(2,1)} %all-gather.2.cloned.1.call-done, s32[]{:T(128)S(6)} %select_n.97), kind=kOutput, calls=%fused_computation.14 | convolution fusion | flops 2417098752 | bytes 7077892 | tf_op jit(solution)/shard_map/td,ktc->kdc/dot_general | solution.py:283
  279.3 4.4 %fusion.15 = bf16[3,512,768]{1,2,0:T(8,128)(2,1)S(1)} fusion(bf16[3,1024,512]{2,1,0:T(8,128)(2,1)S(1)} %copy-done, bf16[1024,6144]{1,0:T(8,128)(2,1)} %all-gather.2.cloned.1.call-done, s32[]{:T(128)S(6)} %select_n.94), kind=kOutput, calls=%fused_computation.33 | convolution fusion | flops 2415919104 | bytes 7077892 | tf_op jit(solution)/shard_map/td,ktc->kdc/dot_general | solution.py:283
  283.7 38.3 %collective-permute-done.15 = bf16[3,768,512]{2,1,0:T(8,128)(2,1)S(1)} collective-permute-done((bf16[3,768,512]{2,1,0:T(8,128)(2,1)}, bf16[3,768,512]{2,1,0:T(8,128)(2,1)S(1)}, u32[]{:S(2)}, u32[]{:S(2)}) %collective-permute-start.15) | collective-permute-done | bytes 2359328 | tf_op jit(solution)/shard_map/ppermute | solution.py:14
  323.1 4.6 %fusion.11 = bf16[3,512,768]{1,2,0:T(8,128)(2,1)S(1)} fusion(bf16[3,1024,512]{2,1,0:T(8,128)(2,1)S(1)} %copy-done, bf16[1024,6144]{1,0:T(8,128)(2,1)} %all-gather.2.cloned.1.call-done, s32[]{:T(128)S(6)} %select_n.95), kind=kOutput, calls=%fused_computation.29 | convolution fusion | flops 2415919104 | bytes 7077892 | tf_op jit(solution)/shard_map/td,ktc->kdc/dot_general | solution.py:283
  331.2 4.4 %fusion.18 = bf16[3,512,768]{1,2,0:T(8,128)(2,1)S(1)} fusion(bf16[3,1024,512]{2,1,0:T(8,128)(2,1)S(1)} %copy-done, bf16[1024,6144]{1,0:T(8,128)(2,1)} %all-gather.2.cloned.1.call-done, s32[]{:T(128)S(6)} %select_n.93), kind=kOutput, calls=%fused_computation.36 | convolution fusion | flops 2415919104 | bytes 7077892 | tf_op jit(solution)/shard_map/td,ktc->kdc/dot_general | solution.py:283
  335.6 4.4 %fusion.21 = bf16[3,512,768]{1,2,0:T(8,128)(2,1)S(1)} fusion(bf16[3,1024,512]{2,1,0:T(8,128)(2,1)S(1)} %copy-done, bf16[1024,6144]{1,0:T(8,128)(2,1)} %all-gather.2.cloned.1.call-done, s32[]{:T(128)S(6)} %select_n.92), kind=kOutput, calls=%fused_computation.39 | convolution fusion | flops 2415919104 | bytes 7077892 | tf_op jit(solution)/shard_map/td,ktc->kdc/dot_general | solution.py:283
  340.0 32.6 %collective-permute-done.17 = bf16[3,768,512]{2,1,0:T(8,128)(2,1)S(1)} collective-permute-done((bf16[3,768,512]{2,1,0:T(8,128)(2,1)S(1)}, bf16[3,768,512]{2,1,0:T(8,128)(2,1)S(1)}, u32[]{:S(2)}, u32[]{:S(2)}) %collective-permute-start.17) | collective-permute-done | bytes 2359328 | tf_op jit(solution)/shard_map/ppermute | solution.py:14
  372.6 4.4 %collective-permute-done.16 = bf16[3,768,512]{2,1,0:T(8,128)(2,1)S(1)} collective-permute-done((bf16[3,768,512]{2,1,0:T(8,128)(2,1)S(1)}, bf16[3,768,512]{2,1,0:T(8,128)(2,1)S(1)}, u32[]{:S(2)}, u32[]{:S(2)}) %collective-permute-start.16) | collective-permute-done | bytes 2359328 | tf_op jit(solution)/shard_map/ppermute | solution.py:14
  378.1 38.0 %collective-permute-done.12 = bf16[3,768,512]{2,1,0:T(8,128)(2,1)S(1)} collective-permute-done((bf16[3,768,512]{2,1,0:T(8,128)(2,1)S(1)}, bf16[3,768,512]{2,1,0:T(8,128)(2,1)S(1)}, u32[]{:S(2)}, u32[]{:S(2)}) %collective-permute-start.12) | collective-permute-done | bytes 2359328 | tf_op jit(solution)/shard_map/ppermute | solution.py:14
  (120 shorter events, 61.5 us)
Async XLA Ops:
  7.2 8.5 %copy-start.7 = (s32[4]{0:T(128)S(1)}, s32[4]{0:T(128)}, u32[]{:S(2)}) copy-start(s32[4]{0:T(128)} %param.9) | copy-start | bytes 52
  7.2 8.7 %copy-start.6 = (f32[4,1024]{1,0:T(4,128)S(1)}, f32[4,1024]{1,0:T(4,128)}, u32[]{:S(2)}) copy-start(f32[4,1024]{1,0:T(4,128)} %param.8) | copy-start | bytes 49156
  7.2 134.0 %all-gather.2.cloned.1.call-start = ((), (), s32[]{:S(2)}) async-start(), calls=%async_computation.1 | async-start | bytes 14155776 | tf_op jit(solution)/shard_map/all_gather | solution.py:200
  7.9 411.7 %reduce-scatter.2.cloned.1.call-start = ((), (), s32[]{:S(2)}) async-start(), calls=%async_computation.2 | async-start | bytes 14155776 | tf_op jit(solution)/shard_map/reduce_scatter | solution.py:310
  11.2 54.5 %collective-permute-start = (bf16[3,768,512]{2,1,0:T(8,128)(2,1)}, bf16[3,768,512]{2,1,0:T(8,128)(2,1)}, u32[]{:S(2)}, u32[]{:S(2)}) collective-permute-start(bf16[3,768,512]{2,1,0:T(8,128)(2,1)} %slice.56), channel_id=1, source_target_pairs={{0,8},{8,0},{16,24},{24,16},{1,9},{9,1},{17,25},{25,17},{2,10},{10... | collective-permute-start | bytes 7077896 | tf_op jit(solution)/shard_map/ppermute | solution.py:14
  14.1 125.2 %collective-permute-start.3 = (bf16[3,768,512]{2,1,0:T(8,128)(2,1)}, bf16[3,768,512]{2,1,0:T(8,128)(2,1)S(1)}, u32[]{:S(2)}, u32[]{:S(2)}) collective-permute-start(bf16[3,768,512]{2,1,0:T(8,128)(2,1)} %slice.56), channel_id=1, source_target_pairs={{0,16},{8,24},{16,0},{24,8},{1,17},{9,25},{17,1},{25,9},{2,18},{10... | collective-permute-start | bytes 7077896 | tf_op jit(solution)/shard_map/ppermute | solution.py:14
  21.3 51.1 %slice-start = ((s8[4718592]{0:T(1024)(128)(4,1)}), s8[4194304]{0:T(1024)(128)(4,1)S(1)}, s32[]{:S(2)}) async-start(s8[4718592]{0:T(1024)(128)(4,1)} %bitcast.119), calls=%async_computation.3 | async-start | bytes 8388608
  21.4 51.0 %slice-start.1 = ((s8[4718592]{0:T(1024)(128)(4,1)}), s8[524288]{0:T(1024)(128)(4,1)S(1)}, s32[]{:S(2)}) async-start(s8[4718592]{0:T(1024)(128)(4,1)} %bitcast.119), calls=%async_computation.4 | async-start | bytes 1048576
  76.6 54.5 %collective-permute-start.1 = (bf16[3,768,512]{2,1,0:T(8,128)(2,1)}, bf16[3,768,512]{2,1,0:T(8,128)(2,1)}, u32[]{:S(2)}, u32[]{:S(2)}) collective-permute-start(bf16[3,768,512]{2,1,0:T(8,128)(2,1)} %get-tuple-element.46), channel_id=1, source_target_pairs={{0,16},{8,24},{16,0},{24,8},{1,17},{9,25},{17,1},{25,9},{2,18},{10... | collective-permute-start | bytes 7077896 | tf_op jit(solution)/shard_map/ppermute | solution.py:14
  78.6 57.5 %collective-permute-start.2 = (bf16[3,768,512]{2,1,0:T(8,128)(2,1)}, bf16[3,768,512]{2,1,0:T(8,128)(2,1)}, u32[]{:S(2)}, u32[]{:S(2)}) collective-permute-start(bf16[3,768,512]{2,1,0:T(8,128)(2,1)} %get-tuple-element.46), channel_id=1, source_target_pairs={{0,8},{8,0},{16,24},{24,16},{1,9},{9,1},{17,25},{25,17},{2,10},{10... | collective-permute-start | bytes 7077896 | tf_op jit(solution)/shard_map/ppermute | solution.py:14
  84.0 103.6 %collective-permute-start.8 = (bf16[3,768,512]{2,1,0:T(8,128)(2,1)}, bf16[3,768,512]{2,1,0:T(8,128)(2,1)}, u32[]{:S(2)}, u32[]{:S(2)}) collective-permute-start(bf16[3,768,512]{2,1,0:T(8,128)(2,1)} %collective-permute-done), channel_id=1, source_target_pairs={{0,16},{8,24},{16,0},{24,8},{1,17},{9,25},{17,1},{25,9},{2,18},{10... | collective-permute-start | bytes 7077896 | tf_op jit(solution)/shard_map/ppermute | solution.py:14
  131.1 51.7 %collective-permute-start.7 = (bf16[3,768,512]{2,1,0:T(8,128)(2,1)}, bf16[3,768,512]{2,1,0:T(8,128)(2,1)}, u32[]{:S(2)}, u32[]{:S(2)}) collective-permute-start(bf16[3,768,512]{2,1,0:T(8,128)(2,1)} %collective-permute-done.1), channel_id=1, source_target_pairs={{0,8},{8,0},{16,24},{24,16},{1,9},{9,1},{17,25},{25,17},{2,10},{10... | collective-permute-start | bytes 7077896 | tf_op jit(solution)/shard_map/ppermute | solution.py:14
  139.4 3.7 copy-start.1
  143.1 6.8 %slice-start.2 = ((s8[4718592]{0:T(1024)(128)(4,1)}), s8[4194304]{0:T(1024)(128)(4,1)S(1)}, s32[]{:S(2)}) async-start(s8[4718592]{0:T(1024)(128)(4,1)} %bitcast.123), calls=%async_computation.5 | async-start | bytes 8388608
  145.0 4.8 %slice-start.3 = ((s8[4718592]{0:T(1024)(128)(4,1)}), s8[524288]{0:T(1024)(128)(4,1)S(1)}, s32[]{:S(2)}) async-start(s8[4718592]{0:T(1024)(128)(4,1)} %bitcast.123), calls=%async_computation.6 | async-start | bytes 1048576
  177.9 34.6 %collective-permute-start.6 = (f32[4,128]{0,1:T(8,128)S(1)}, f32[4,128]{0,1:T(8,128)S(1)}, u32[]{:S(2)}, u32[]{:S(2)}) collective-permute-start(f32[4,128]{0,1:T(8,128)S(1)} %broadcast_in_dim.147), channel_id=1, source_target_pairs={{0,24},{8,16},{16,8},{24,0},{1,25},{9,17},{17,9},{25,1},{2,26},{10... | collective-permute-start | bytes 6152 | tf_op jit(solution)/shard_map/ppermute | solution.py:14
  179.4 33.8 %collective-permute-start.5 = (f32[4,128]{0,1:T(8,128)S(1)}, f32[4,128]{0,1:T(8,128)S(1)}, u32[]{:S(2)}, u32[]{:S(2)}) collective-permute-start(f32[4,128]{0,1:T(8,128)S(1)} %broadcast_in_dim.147), channel_id=1, source_target_pairs={{0,16},{8,24},{16,0},{24,8},{1,17},{9,25},{17,1},{25,9},{2,18},{10... | collective-permute-start | bytes 6152 | tf_op jit(solution)/shard_map/ppermute | solution.py:14
  179.9 33.4 %collective-permute-start.4 = (f32[4,128]{0,1:T(8,128)S(1)}, f32[4,128]{0,1:T(8,128)S(1)}, u32[]{:S(2)}, u32[]{:S(2)}) collective-permute-start(f32[4,128]{0,1:T(8,128)S(1)} %broadcast_in_dim.147), channel_id=1, source_target_pairs={{0,8},{8,0},{16,24},{24,16},{1,9},{9,1},{17,25},{25,17},{2,10},{10... | collective-permute-start | bytes 6152 | tf_op jit(solution)/shard_map/ppermute | solution.py:14
  203.3 11.0 %collective-permute-start.9 = (bf16[2,4,128,128]{3,2,1,0:T(8,128)(2,1)}, bf16[2,4,128,128]{3,2,1,0:T(8,128)(2,1)S(1)}, u32[]{:S(2)}, u32[]{:S(2)}) collective-permute-start(bf16[2,4,128,128]{3,2,1,0:T(8,128)(2,1)} %get-tuple-element.32.rest_0_), channel_id=1, source_target_pairs={{0,8},{8,0},{16,24},{24,16},{1,9},{9,1},{17,25},{25,17},{2,10},{10... | collective-permute-start | bytes 786440 | tf_op jit(solution)/shard_map/ppermute | solution.py:14
  204.9 9.4 %collective-permute-start.10 = (bf16[2,4,128,128]{3,2,1,0:T(8,128)(2,1)}, bf16[2,4,128,128]{3,2,1,0:T(8,128)(2,1)S(1)}, u32[]{:S(2)}, u32[]{:S(2)}) collective-permute-start(bf16[2,4,128,128]{3,2,1,0:T(8,128)(2,1)} %get-tuple-element.32.rest_0_), channel_id=1, source_target_pairs={{0,16},{8,24},{16,0},{24,8},{1,17},{9,25},{17,1},{25,9},{2,18},{10... | collective-permute-start | bytes 786440 | tf_op jit(solution)/shard_map/ppermute | solution.py:14
  209.2 3.4 copy-start.2
  212.6 7.3 %collective-permute-start.11 = (bf16[2,4,128,128]{3,2,1,0:T(8,128)(2,1)S(1)}, bf16[2,4,128,128]{3,2,1,0:T(8,128)(2,1)S(1)}, u32[]{:S(2)}, u32[]{:S(2)}) collective-permute-start(bf16[2,4,128,128]{3,2,1,0:T(8,128)(2,1)S(1)} %copy-done.2), channel_id=1, source_target_pairs={{0,24},{8,16},{16,8},{24,0},{1,25},{9,17},{17,9},{25,1},{2,26},{10... | collective-permute-start | bytes 786440 | tf_op jit(solution)/shard_map/ppermute | solution.py:14
  214.3 5.6 %copy-start.3 = (bf16[2,4,128,128]{3,2,1,0:T(8,128)(2,1)}, bf16[2,4,128,128]{3,2,1,0:T(8,128)(2,1)S(1)}, u32[]{:S(2)}) copy-start(bf16[2,4,128,128]{3,2,1,0:T(8,128)(2,1)S(1)} %collective-permute-done.9.rest_1_) | copy-start | bytes 786436
  214.3 5.5 %copy-start.4 = (bf16[2,4,128,128]{3,2,1,0:T(8,128)(2,1)}, bf16[2,4,128,128]{3,2,1,0:T(8,128)(2,1)S(1)}, u32[]{:S(2)}) copy-start(bf16[2,4,128,128]{3,2,1,0:T(8,128)(2,1)S(1)} %collective-permute-done.10.rest_2_) | copy-start | bytes 786436
  219.8 0.7 copy-start.5
  231.6 6.6 %copy-start = (bf16[3,1024,512]{2,1,0:T(8,128)(2,1)S(1)}, bf16[3,1024,512]{2,1,0:T(8,128)(2,1)}, u32[]{:S(2)}) copy-start(bf16[3,1024,512]{2,1,0:T(8,128)(2,1)} %shard_map.69.gradient_ref) | copy-start | bytes 9437188
  267.6 54.5 %collective-permute-start.15 = (bf16[3,768,512]{2,1,0:T(8,128)(2,1)}, bf16[3,768,512]{2,1,0:T(8,128)(2,1)S(1)}, u32[]{:S(2)}, u32[]{:S(2)}) collective-permute-start(bf16[3,768,512]{2,1,0:T(8,128)(2,1)} %convert_bitcast_fusion.2), channel_id=1, source_target_pairs={{0,16},{8,24},{16,0},{24,8},{1,17},{9,25},{17,1},{25,9},{2,18},{10... | collective-permute-start | bytes 7077896 | tf_op jit(solution)/shard_map/ppermute | solution.py:14
  268.6 60.9 %collective-permute-start.13 = (bf16[3,768,512]{2,1,0:T(8,128)(2,1)}, bf16[3,768,512]{2,1,0:T(8,128)(2,1)S(1)}, u32[]{:S(2)}, u32[]{:S(2)}) collective-permute-start(bf16[3,768,512]{2,1,0:T(8,128)(2,1)} %convert_bitcast_fusion.3), channel_id=1, source_target_pairs={{0,8},{8,0},{16,24},{24,16},{1,9},{9,1},{17,25},{25,17},{2,10},{10... | collective-permute-start | bytes 7077896 | tf_op jit(solution)/shard_map/ppermute | solution.py:14
  278.1 94.6 %collective-permute-start.17 = (bf16[3,768,512]{2,1,0:T(8,128)(2,1)S(1)}, bf16[3,768,512]{2,1,0:T(8,128)(2,1)S(1)}, u32[]{:S(2)}, u32[]{:S(2)}) collective-permute-start(bf16[3,768,512]{2,1,0:T(8,128)(2,1)S(1)} %convert_bitcast_fusion), channel_id=1, source_target_pairs={{0,16},{8,24},{16,0},{24,8},{1,17},{9,25},{17,1},{25,9},{2,18},{10... | collective-permute-start | bytes 7077896 | tf_op jit(solution)/shard_map/ppermute | solution.py:14
  322.8 54.3 %collective-permute-start.16 = (bf16[3,768,512]{2,1,0:T(8,128)(2,1)S(1)}, bf16[3,768,512]{2,1,0:T(8,128)(2,1)S(1)}, u32[]{:S(2)}, u32[]{:S(2)}) collective-permute-start(bf16[3,768,512]{2,1,0:T(8,128)(2,1)S(1)} %add_convert_fusion.1), channel_id=1, source_target_pairs={{0,8},{8,0},{16,24},{24,16},{1,9},{9,1},{17,25},{25,17},{2,10},{10... | collective-permute-start | bytes 7077896 | tf_op jit(solution)/shard_map/ppermute | solution.py:14
  327.7 88.4 %collective-permute-start.12 = (bf16[3,768,512]{2,1,0:T(8,128)(2,1)S(1)}, bf16[3,768,512]{2,1,0:T(8,128)(2,1)S(1)}, u32[]{:S(2)}, u32[]{:S(2)}) collective-permute-start(bf16[3,768,512]{2,1,0:T(8,128)(2,1)S(1)} %convert_bitcast_fusion.1), channel_id=1, source_target_pairs={{0,8},{8,0},{16,24},{24,16},{1,9},{9,1},{17,25},{25,17},{2,10},{10... | collective-permute-start | bytes 7077896 | tf_op jit(solution)/shard_map/ppermute | solution.py:14
  330.2 85.9 %collective-permute-start.14 = (bf16[3,768,512]{2,1,0:T(8,128)(2,1)S(1)}, bf16[3,768,512]{2,1,0:T(8,128)(2,1)S(1)}, u32[]{:S(2)}, u32[]{:S(2)}) collective-permute-start(bf16[3,768,512]{2,1,0:T(8,128)(2,1)S(1)} %add_convert_fusion.3), channel_id=1, source_target_pairs={{0,16},{8,24},{16,0},{24,8},{1,17},{9,25},{17,1},{25,9},{2,18},{10... | collective-permute-start | bytes 7077896 | tf_op jit(solution)/shard_map/ppermute | solution.py:14
Sparse Core Ops, SparseCore 0:
  9.6 119.4 all-gather.1
  267.7 128.9 reduce-scatter.1

commit v4 on v3

--- a/solution.py
+++ b/solution.py
@@ -231,7 +231,7 @@
             whole = lax.dynamic_update_slice_in_dim(whole, block, owner * rows + first, axis=1)
         return whole
 
-    early, late = blocks_w[:6], blocks_w[6:]
+    early, late = blocks_w[:4], blocks_w[4:]
     weights_all = place_rows(weights_all, early)
     features, weights_all, from_start, to_end, pair_weight = lax.optimization_barrier(
         (features, weights_all, from_start, to_end, pair_weight)

time: 430 us -> 442 us (1.028)
  waiting for transfers between devices: 209 us -> 218 us
    ppermute x18, waiting for transfers between devices: 208 us -> 217 us  [hop(): lax.ppermute(array, axis, [(i, i ^ flip) for i in range(lax.axis_size(axi...]
  transfers between devices with their start and end apart: 20 -> 20, of which waited for: 9 -> 8; matrix products, arithmetic and copies ran while one was open for 30% -> 29% of each run, Pallas kernels for 2% -> 2%
where the time goes in v4:
time: 442 us; the launch traced here: 438 us
  waiting for transfers between devices  218 us (49%)
  matrix products  76.5 us (17%)
  Pallas kernels  42 us (10%)
  local copies, waits for them, and re-layouts  39.3 us (9%)
  other arithmetic  24.3 us (5%)
  starting transfers between devices  23.6 us (5%)
  between operations  14.6 us (3%)
    ppermute x18, waiting for transfers between devices, hop(): lax.ppermute(array, axis, [(i, i ^ flip) for i in range(lax.axis_size(axi...  217 us
    dot_general x8, matrix products, weight_partial(): jnp.einsum('td,ktc->kdc', feature_rows(owner, first, count), gradient, pr...  38.8 us
    dot_general x8, matrix products, body(): jnp.einsum('td,kdc->ktc', feature_rows(owner, first, block.shape[1]), blo...  37.7 us
    pallas_call x1, Pallas kernels, input_partial(): pl.pallas_call(input_kernel, grid=(columns // tile,), in_specs=[pl.BlockS...  24.2 us
    ppermute x18, starting transfers between devices, hop(): lax.ppermute(array, axis, [(i, i ^ flip) for i in range(lax.axis_size(axi...  23.6 us
    dynamic_update_slice x7, local copies, waits for them, and re-layouts, place_rows(): lax.dynamic_update_slice_in_dim(whole, block, owner * rows + first, axis=1)  21.3 us
    pallas_call x1, Pallas kernels, body(): pl.pallas_call(gradient_kernel, grid=(heads_here,), in_specs=[pl.BlockSpe...  11.1 us
    add x4, other arithmetic, body(): lax.optimization_barrier(projected) + piece  8.84 us
  transfers between devices with their start and end apart: 20, of which 8 were waited for; matrix products, arithmetic and copies ran while one was open for 29% of the time, Pallas kernels for 2%

profile of v4, /device:TPU:0, one launch (start us, length us, event | category | flops | bytes accessed | tf_op | source)
XLA Modules:
  0.0 438.3 jit_solution(17004477696149148324)
XLA Ops:
  15.9 4.8 %reduce-window.6 = f32[4,4,2,128]{3,2,1,0:T(2,128)S(1)} reduce-window(f32[4,4,2,128]{3,2,1,0:T(2,128)S(1)} %reshape.321, f32[]{:T(128)} %constant.38.clone.1), window={size=1x1x1x128 pad=0_0x0_0x0_0x127_0}, to_apply=%region_2.0 | reduce-window | flops 520192 | bytes 32772 | tf_op jit(solution)/shard_map/reduce-window
  21.4 44.3 %collective-permute-done = bf16[3,768,512]{2,1,0:T(8,128)(2,1)} collective-permute-done((bf16[3,768,512]{2,1,0:T(8,128)(2,1)}, bf16[3,768,512]{2,1,0:T(8,128)(2,1)}, u32[]{:S(2)}, u32[]{:S(2)}) %collective-permute-start) | collective-permute-done | bytes 2359328 | tf_op jit(solution)/shard_map/ppermute | solution.py:14
  65.7 6.7 %broadcast_in_dim.138 = bf16[3,6144,512]{2,1,0:T(8,128)(2,1)} broadcast(bf16[]{:T(256)} %constant.16.clone.1), dimensions={} | broadcast | bytes 18874370 | tf_op jit(solution)/shard_map/broadcast_in_dim | solution.py:227
  84.4 3.3 constant_dynamic-update-slice_fusion.5
  87.7 43.5 %collective-permute-done.1 = bf16[3,768,512]{2,1,0:T(8,128)(2,1)} collective-permute-done((bf16[3,768,512]{2,1,0:T(8,128)(2,1)}, bf16[3,768,512]{2,1,0:T(8,128)(2,1)}, u32[]{:S(2)}, u32[]{:S(2)}) %collective-permute-start.1) | collective-permute-done | bytes 2359328 | tf_op jit(solution)/shard_map/ppermute | solution.py:14
  140.1 4.8 %convolution_bitcast_fusion = f32[3,1024,512]{2,1,0:T(8,128)S(1)} fusion(bf16[1024,6144]{1,0:T(8,128)(2,1)} %all-gather.2.cloned.1.call-done, s32[]{:T(128)S(6)} %select_n.92, bf16[3,1536,512]{2,1,0:T(8,128)(2,1)} %bitcast.118), kind=kOutput, calls=%fused_computation.13 | convolution fusion | flops 2415919104 | bytes 10223620 | tf_op jit(solution)/shard_map/td,kdc->ktc/dot_general | solution.py:241
  144.9 4.0 bitcast_add_fusion.6
  149.0 4.8 %bitcast_add_fusion.5 = f32[3,1024,512]{2,1,0:T(8,128)S(1)} fusion(f32[3,1024,512]{2,1,0:T(8,128)S(1)} %bitcast_add_fusion.6, bf16[3,768,512]{2,1,0:T(8,128)(2,1)} %collective-permute-done, bf16[1024,6144]{1,0:T(8,128)(2,1)} %all-gather.2.cloned.1.call-done, s32[]{:T(128)S(6)} %select_n.94), kind=kOutput, calls=%fused_computation.5 | convolution fusion | flops 2417491968 | bytes 16515076 | tf_op jit(solution)/shard_map/td,kdc->ktc/dot_general | solution.py:241
  153.8 4.8 %fusion.13 = f32[1024,3,512]{2,0,1:T(8,128)S(1)} fusion(bf16[3,768,512]{2,1,0:T(8,128)(2,1)} %collective-permute-done.1, bf16[1024,6144]{1,0:T(8,128)(2,1)} %all-gather.2.cloned.1.call-done, s32[]{:T(128)S(6)} %select_n.95), kind=kOutput, calls=%fused_computation.31 | convolution fusion | flops 2415919104 | bytes 10223620 | tf_op jit(solution)/shard_map/td,kdc->ktc/dot_general | solution.py:241
  160.1 4.8 %fusion.9 = f32[1024,3,512]{2,0,1:T(8,128)S(1)} fusion(bf16[3,768,512]{2,1,0:T(8,128)(2,1)} %collective-permute-done.2, bf16[1024,6144]{1,0:T(8,128)(2,1)} %all-gather.2.cloned.1.call-done, s32[]{:T(128)S(6)} %select_n.99), kind=kOutput, calls=%fused_computation.27 | convolution fusion | flops 2415919104 | bytes 10223620 | tf_op jit(solution)/shard_map/td,kdc->ktc/dot_general | solution.py:241
  166.4 5.0 %fusion.6 = f32[1024,3,512]{2,0,1:T(8,128)S(1)} fusion(bf16[3,768,512]{2,1,0:T(8,128)(2,1)} %collective-permute-done.3, bf16[1024,6144]{1,0:T(8,128)(2,1)} %all-gather.2.cloned.1.call-done, s32[]{:T(128)S(6)} %select_n.100), kind=kOutput, calls=%fused_computation.24 | convolution fusion | flops 2415919104 | bytes 10223620 | tf_op jit(solution)/shard_map/td,kdc->ktc/dot_general | solution.py:241
  176.5 10.0 %collective-permute-done.7 = bf16[3,768,512]{2,1,0:T(8,128)(2,1)} collective-permute-done((bf16[3,768,512]{2,1,0:T(8,128)(2,1)}, bf16[3,768,512]{2,1,0:T(8,128)(2,1)}, u32[]{:S(2)}, u32[]{:S(2)}) %collective-permute-start.7) | collective-permute-done | bytes 2359328 | tf_op jit(solution)/shard_map/ppermute | solution.py:14
  186.5 4.8 %bitcast_add_fusion.1 = f32[3,1024,512]{2,1,0:T(8,128)S(1)} fusion(f32[3,1024,512]{2,1,0:T(8,128)S(1)} %bitcast_add_fusion.2, bf16[3,768,512]{2,1,0:T(8,128)(2,1)} %collective-permute-done.7, bf16[1024,6144]{1,0:T(8,128)(2,1)} %all-gather.2.cloned.1.call-done, s32[]{:T(128)S(6)} %select_n.107), kind=kOutput, calls=%fused_computation.1 | convolution fusion | flops 2417491968 | bytes 16515076 | tf_op jit(solution)/shard_map/td,kdc->ktc/dot_general | solution.py:241
  191.4 4.8 %fusion.1 = f32[1024,3,512]{2,0,1:T(8,128)S(1)} fusion(bf16[3,768,512]{2,1,0:T(8,128)(2,1)} %collective-permute-done.8, bf16[1024,6144]{1,0:T(8,128)(2,1)} %all-gather.2.cloned.1.call-done, s32[]{:T(128)S(6)} %select_n.108), kind=kOutput, calls=%fused_computation.19 | convolution fusion | flops 2415919104 | bytes 10223620 | tf_op jit(solution)/shard_map/td,kdc->ktc/dot_general | solution.py:241
  196.1 4.2 bitcast_add_fusion.proj_ref
  200.3 6.7 %shard_map.68 = (f32[4,4,128,128]{3,2,1,0:T(8,128)}, f32[4,4,128,128]{3,2,1,0:T(8,128)}, bf16[2,4,128,128]{3,2,1,0:T(8,128)(2,1)}) custom-call(f32[3,1024,512]{2,1,0:T(8,128)} %bitcast_add_fusion.proj_ref, bf16[1024,512]{1,0:T(8,128)(2,1)} %up_ref.3, f32[4,1024,128]{2,1,0:T(8,128)} %broadcast_in_dim.141.start_ref, f32[4,1024,128]{2,1,0:T(8,128)} %broadcast_in_dim.143.end_ref), custom_call_target="tpu_custom_call" | custom-call | tf_op jit(solution)/shard_map/pallas_call | solution.py:259
  218.7 3.4 constant_dynamic-update-slice_fusion.weight_ref
  224.5 4.9 %collective-permute-done.11.rest_3_ = bf16[2,4,128,128]{3,2,1,0:T(8,128)(2,1)S(1)} collective-permute-done((bf16[2,4,128,128]{3,2,1,0:T(8,128)(2,1)S(1)}, bf16[2,4,128,128]{3,2,1,0:T(8,128)(2,1)S(1)}, u32[]{:S(2)}, u32[]{:S(2)}) %collective-permute-start.11) | collective-permute-done | bytes 262176 | tf_op jit(solution)/shard_map/ppermute | solution.py:14
  230.1 11.1 %shard_map.69.gradient_ref = bf16[3,1024,512]{2,1,0:T(8,128)(2,1)} custom-call(f32[2,4,4]{2,1,0:T(4,128)} %pad_maximum_fusion.weight_ref, f32[3,1024,512]{2,1,0:T(8,128)} %bitcast_add_fusion.proj_ref, bf16[1024,512]{1,0:T(8,128)(2,1)} %up_ref.3, f32[4,1024,128]{2,1,0:T(8,128)} %broadcast_in_dim.141.start_ref, f32[4,1024,128]{2,1,0:T(8,128)} %broadcast_in_dim.143.end_ref, ...), custom_call_target="tpu_custom_call" | custom-call | tf_op jit(solution)/shard_map/pallas_call | solution.py:272
  241.2 6.6 %convert_bitcast_fusion.3 = bf16[3,768,512]{2,1,0:T(8,128)(2,1)} fusion(bf16[3,1024,512]{2,1,0:T(8,128)(2,1)} %shard_map.69.gradient_ref, bf16[1024,6144]{1,0:T(8,128)(2,1)} %all-gather.2.cloned.1.call-done, s32[]{:T(128)S(6)} %select_n.107), kind=kOutput, calls=%fused_computation.17 | convolution fusion | flops 2417098752 | bytes 7077892 | tf_op jit(solution)/shard_map/td,ktc->kdc/dot_general | solution.py:283
  247.7 5.3 %convert_bitcast_fusion.2 = bf16[3,768,512]{2,1,0:T(8,128)(2,1)} fusion(bf16[3,1024,512]{2,1,0:T(8,128)(2,1)S(1)} %copy-done, bf16[1024,6144]{1,0:T(8,128)(2,1)} %all-gather.2.cloned.1.call-done, s32[]{:T(128)S(6)} %select_n.108), kind=kOutput, calls=%fused_computation.16 | convolution fusion | flops 2417098752 | bytes 7077892 | tf_op jit(solution)/shard_map/td,ktc->kdc/dot_general | solution.py:283
  253.1 24.2 %shard_map.70 = bf16[1024,6144]{1,0:T(8,128)(2,1)} custom-call(bf16[3,1024,512]{2,1,0:T(8,128)(2,1)S(1)} %copy-done, bf16[3,6144,512]{2,1,0:T(8,128)(2,1)} %constant_dynamic-update-slice_fusion.weight_ref), custom_call_target="tpu_custom_call" | custom-call | flops 1 | bytes 1 | tf_op jit(solution)/shard_map/pallas_call | solution.py:294
  279.3 4.4 %convert_bitcast_fusion.1 = bf16[3,768,512]{2,1,0:T(8,128)(2,1)S(1)} fusion(bf16[3,1024,512]{2,1,0:T(8,128)(2,1)S(1)} %copy-done, bf16[1024,6144]{1,0:T(8,128)(2,1)} %all-gather.2.cloned.1.call-done, s32[]{:T(128)S(6)} %select_n.99), kind=kOutput, calls=%fused_computation.15 | convolution fusion | flops 2417098752 | bytes 7077892 | tf_op jit(solution)/shard_map/td,ktc->kdc/dot_general | solution.py:283
  283.7 4.7 %convert_bitcast_fusion = bf16[3,768,512]{2,1,0:T(8,128)(2,1)S(1)} fusion(bf16[3,1024,512]{2,1,0:T(8,128)(2,1)S(1)} %copy-done, bf16[1024,6144]{1,0:T(8,128)(2,1)} %all-gather.2.cloned.1.call-done, s32[]{:T(128)S(6)} %select_n.100), kind=kOutput, calls=%fused_computation.14 | convolution fusion | flops 2417098752 | bytes 7077892 | tf_op jit(solution)/shard_map/td,ktc->kdc/dot_general | solution.py:283
  289.2 4.4 %fusion.15 = bf16[3,512,768]{1,2,0:T(8,128)(2,1)S(1)} fusion(bf16[3,1024,512]{2,1,0:T(8,128)(2,1)S(1)} %copy-done, bf16[1024,6144]{1,0:T(8,128)(2,1)} %all-gather.2.cloned.1.call-done, s32[]{:T(128)S(6)} %select_n.94), kind=kOutput, calls=%fused_computation.33 | convolution fusion | flops 2415919104 | bytes 7077892 | tf_op jit(solution)/shard_map/td,ktc->kdc/dot_general | solution.py:283
  293.6 38.1 %collective-permute-done.15 = bf16[3,768,512]{2,1,0:T(8,128)(2,1)S(1)} collective-permute-done((bf16[3,768,512]{2,1,0:T(8,128)(2,1)}, bf16[3,768,512]{2,1,0:T(8,128)(2,1)S(1)}, u32[]{:S(2)}, u32[]{:S(2)}) %collective-permute-start.15) | collective-permute-done | bytes 2359328 | tf_op jit(solution)/shard_map/ppermute | solution.py:14
  333.1 4.6 %fusion.11 = bf16[3,512,768]{1,2,0:T(8,128)(2,1)S(1)} fusion(bf16[3,1024,512]{2,1,0:T(8,128)(2,1)S(1)} %copy-done, bf16[1024,6144]{1,0:T(8,128)(2,1)} %all-gather.2.cloned.1.call-done, s32[]{:T(128)S(6)} %select_n.95), kind=kOutput, calls=%fused_computation.29 | convolution fusion | flops 2415919104 | bytes 7077892 | tf_op jit(solution)/shard_map/td,ktc->kdc/dot_general | solution.py:283
  341.5 4.4 %fusion.18 = bf16[3,512,768]{1,2,0:T(8,128)(2,1)S(1)} fusion(bf16[3,1024,512]{2,1,0:T(8,128)(2,1)S(1)} %copy-done, bf16[1024,6144]{1,0:T(8,128)(2,1)} %all-gather.2.cloned.1.call-done, s32[]{:T(128)S(6)} %select_n.93), kind=kOutput, calls=%fused_computation.36 | convolution fusion | flops 2415919104 | bytes 7077892 | tf_op jit(solution)/shard_map/td,ktc->kdc/dot_general | solution.py:283
  345.9 4.4 %fusion.21 = bf16[3,512,768]{1,2,0:T(8,128)(2,1)S(1)} fusion(bf16[3,1024,512]{2,1,0:T(8,128)(2,1)S(1)} %copy-done, bf16[1024,6144]{1,0:T(8,128)(2,1)} %all-gather.2.cloned.1.call-done, s32[]{:T(128)S(6)} %select_n.92), kind=kOutput, calls=%fused_computation.39 | convolution fusion | flops 2415919104 | bytes 7077892 | tf_op jit(solution)/shard_map/td,ktc->kdc/dot_general | solution.py:283
  350.3 32.0 %collective-permute-done.17 = bf16[3,768,512]{2,1,0:T(8,128)(2,1)S(1)} collective-permute-done((bf16[3,768,512]{2,1,0:T(8,128)(2,1)S(1)}, bf16[3,768,512]{2,1,0:T(8,128)(2,1)S(1)}, u32[]{:S(2)}, u32[]{:S(2)}) %collective-permute-start.17) | collective-permute-done | bytes 2359328 | tf_op jit(solution)/shard_map/ppermute | solution.py:14
  382.3 4.4 %collective-permute-done.16 = bf16[3,768,512]{2,1,0:T(8,128)(2,1)S(1)} collective-permute-done((bf16[3,768,512]{2,1,0:T(8,128)(2,1)S(1)}, bf16[3,768,512]{2,1,0:T(8,128)(2,1)S(1)}, u32[]{:S(2)}, u32[]{:S(2)}) %collective-permute-start.16) | collective-permute-done | bytes 2359328 | tf_op jit(solution)/shard_map/ppermute | solution.py:14
  387.8 39.9 %collective-permute-done.12 = bf16[3,768,512]{2,1,0:T(8,128)(2,1)S(1)} collective-permute-done((bf16[3,768,512]{2,1,0:T(8,128)(2,1)S(1)}, bf16[3,768,512]{2,1,0:T(8,128)(2,1)S(1)}, u32[]{:S(2)}, u32[]{:S(2)}) %collective-permute-start.12) | collective-permute-done | bytes 2359328 | tf_op jit(solution)/shard_map/ppermute | solution.py:14
  (118 shorter events, 65.7 us)
Async XLA Ops:
  7.2 8.5 %copy-start.6 = (s32[4]{0:T(128)S(1)}, s32[4]{0:T(128)}, u32[]{:S(2)}) copy-start(s32[4]{0:T(128)} %param.9) | copy-start | bytes 52
  7.2 8.7 %copy-start.5 = (f32[4,1024]{1,0:T(4,128)S(1)}, f32[4,1024]{1,0:T(4,128)}, u32[]{:S(2)}) copy-start(f32[4,1024]{1,0:T(4,128)} %param.8) | copy-start | bytes 49156
  7.2 129.0 %all-gather.2.cloned.1.call-start = ((), (), s32[]{:S(2)}) async-start(), calls=%async_computation.1 | async-start | bytes 14155776 | tf_op jit(solution)/shard_map/all_gather | solution.py:200
  7.9 423.3 %reduce-scatter.2.cloned.1.call-start = ((), (), s32[]{:S(2)}) async-start(), calls=%async_computation.2 | async-start | bytes 14155776 | tf_op jit(solution)/shard_map/reduce_scatter | solution.py:310
  11.2 54.5 %collective-permute-start = (bf16[3,768,512]{2,1,0:T(8,128)(2,1)}, bf16[3,768,512]{2,1,0:T(8,128)(2,1)}, u32[]{:S(2)}, u32[]{:S(2)}) collective-permute-start(bf16[3,768,512]{2,1,0:T(8,128)(2,1)} %slice.56), channel_id=1, source_target_pairs={{0,8},{8,0},{16,24},{24,16},{1,9},{9,1},{17,25},{25,17},{2,10},{10... | collective-permute-start | bytes 7077896 | tf_op jit(solution)/shard_map/ppermute | solution.py:14
  14.2 152.3 %collective-permute-start.3 = (bf16[3,768,512]{2,1,0:T(8,128)(2,1)}, bf16[3,768,512]{2,1,0:T(8,128)(2,1)}, u32[]{:S(2)}, u32[]{:S(2)}) collective-permute-start(bf16[3,768,512]{2,1,0:T(8,128)(2,1)} %slice.56), channel_id=1, source_target_pairs={{0,16},{8,24},{16,0},{24,8},{1,17},{9,25},{17,1},{25,9},{2,18},{10... | collective-permute-start | bytes 7077896 | tf_op jit(solution)/shard_map/ppermute | solution.py:14
  21.3 51.1 %slice-start = ((s8[4718592]{0:T(1024)(128)(4,1)}), s8[4194304]{0:T(1024)(128)(4,1)S(1)}, s32[]{:S(2)}) async-start(s8[4718592]{0:T(1024)(128)(4,1)} %bitcast.119), calls=%async_computation.3 | async-start | bytes 8388608
  21.4 51.0 %slice-start.1 = ((s8[4718592]{0:T(1024)(128)(4,1)}), s8[524288]{0:T(1024)(128)(4,1)S(1)}, s32[]{:S(2)}) async-start(s8[4718592]{0:T(1024)(128)(4,1)} %bitcast.119), calls=%async_computation.4 | async-start | bytes 1048576
  76.7 54.5 %collective-permute-start.1 = (bf16[3,768,512]{2,1,0:T(8,128)(2,1)}, bf16[3,768,512]{2,1,0:T(8,128)(2,1)}, u32[]{:S(2)}, u32[]{:S(2)}) collective-permute-start(bf16[3,768,512]{2,1,0:T(8,128)(2,1)} %get-tuple-element.46), channel_id=1, source_target_pairs={{0,16},{8,24},{16,0},{24,8},{1,17},{9,25},{17,1},{25,9},{2,18},{10... | collective-permute-start | bytes 7077896 | tf_op jit(solution)/shard_map/ppermute | solution.py:14
  82.4 77.8 %collective-permute-start.2 = (bf16[3,768,512]{2,1,0:T(8,128)(2,1)}, bf16[3,768,512]{2,1,0:T(8,128)(2,1)}, u32[]{:S(2)}, u32[]{:S(2)}) collective-permute-start(bf16[3,768,512]{2,1,0:T(8,128)(2,1)} %get-tuple-element.46), channel_id=1, source_target_pairs={{0,8},{8,0},{16,24},{24,16},{1,9},{9,1},{17,25},{25,17},{2,10},{10... | collective-permute-start | bytes 7077896 | tf_op jit(solution)/shard_map/ppermute | solution.py:14
  84.0 107.3 %collective-permute-start.8 = (bf16[3,768,512]{2,1,0:T(8,128)(2,1)}, bf16[3,768,512]{2,1,0:T(8,128)(2,1)}, u32[]{:S(2)}, u32[]{:S(2)}) collective-permute-start(bf16[3,768,512]{2,1,0:T(8,128)(2,1)} %collective-permute-done), channel_id=1, source_target_pairs={{0,16},{8,24},{16,0},{24,8},{1,17},{9,25},{17,1},{25,9},{2,18},{10... | collective-permute-start | bytes 7077896 | tf_op jit(solution)/shard_map/ppermute | solution.py:14
  131.2 55.4 %collective-permute-start.7 = (bf16[3,768,512]{2,1,0:T(8,128)(2,1)}, bf16[3,768,512]{2,1,0:T(8,128)(2,1)}, u32[]{:S(2)}, u32[]{:S(2)}) collective-permute-start(bf16[3,768,512]{2,1,0:T(8,128)(2,1)} %collective-permute-done.1), channel_id=1, source_target_pairs={{0,8},{8,0},{16,24},{24,16},{1,9},{9,1},{17,25},{25,17},{2,10},{10... | collective-permute-start | bytes 7077896 | tf_op jit(solution)/shard_map/ppermute | solution.py:14
  138.1 6.8 %slice-start.2 = ((s8[4718592]{0:T(1024)(128)(4,1)}), s8[4194304]{0:T(1024)(128)(4,1)S(1)}, s32[]{:S(2)}) async-start(s8[4718592]{0:T(1024)(128)(4,1)} %bitcast.123), calls=%async_computation.5 | async-start | bytes 8388608
  140.1 4.8 %slice-start.3 = ((s8[4718592]{0:T(1024)(128)(4,1)}), s8[524288]{0:T(1024)(128)(4,1)S(1)}, s32[]{:S(2)}) async-start(s8[4718592]{0:T(1024)(128)(4,1)} %bitcast.123), calls=%async_computation.6 | async-start | bytes 1048576
  173.0 49.1 %collective-permute-start.6 = (f32[4,128]{0,1:T(8,128)S(1)}, f32[4,128]{0,1:T(8,128)S(1)}, u32[]{:S(2)}, u32[]{:S(2)}) collective-permute-start(f32[4,128]{0,1:T(8,128)S(1)} %broadcast_in_dim.147), channel_id=1, source_target_pairs={{0,24},{8,16},{16,8},{24,0},{1,25},{9,17},{17,9},{25,1},{2,26},{10... | collective-permute-start | bytes 6152 | tf_op jit(solution)/shard_map/ppermute | solution.py:14
  174.6 48.9 %collective-permute-start.5 = (f32[4,128]{0,1:T(8,128)S(1)}, f32[4,128]{0,1:T(8,128)S(1)}, u32[]{:S(2)}, u32[]{:S(2)}) collective-permute-start(f32[4,128]{0,1:T(8,128)S(1)} %broadcast_in_dim.147), channel_id=1, source_target_pairs={{0,16},{8,24},{16,0},{24,8},{1,17},{9,25},{17,1},{25,9},{2,18},{10... | collective-permute-start | bytes 6152 | tf_op jit(solution)/shard_map/ppermute | solution.py:14
  174.8 48.7 %collective-permute-start.4 = (f32[4,128]{0,1:T(8,128)S(1)}, f32[4,128]{0,1:T(8,128)S(1)}, u32[]{:S(2)}, u32[]{:S(2)}) collective-permute-start(f32[4,128]{0,1:T(8,128)S(1)} %broadcast_in_dim.147), channel_id=1, source_target_pairs={{0,8},{8,0},{16,24},{24,16},{1,9},{9,1},{17,25},{25,17},{2,10},{10... | collective-permute-start | bytes 6152 | tf_op jit(solution)/shard_map/ppermute | solution.py:14
  207.0 17.5 %collective-permute-start.9 = (bf16[2,4,128,128]{3,2,1,0:T(8,128)(2,1)}, bf16[2,4,128,128]{3,2,1,0:T(8,128)(2,1)S(1)}, u32[]{:S(2)}, u32[]{:S(2)}) collective-permute-start(bf16[2,4,128,128]{3,2,1,0:T(8,128)(2,1)} %get-tuple-element.32.rest_0_), channel_id=1, source_target_pairs={{0,8},{8,0},{16,24},{24,16},{1,9},{9,1},{17,25},{25,17},{2,10},{10... | collective-permute-start | bytes 786440 | tf_op jit(solution)/shard_map/ppermute | solution.py:14
  208.6 15.9 %collective-permute-start.10 = (bf16[2,4,128,128]{3,2,1,0:T(8,128)(2,1)}, bf16[2,4,128,128]{3,2,1,0:T(8,128)(2,1)S(1)}, u32[]{:S(2)}, u32[]{:S(2)}) collective-permute-start(bf16[2,4,128,128]{3,2,1,0:T(8,128)(2,1)} %get-tuple-element.32.rest_0_), channel_id=1, source_target_pairs={{0,16},{8,24},{16,0},{24,8},{1,17},{9,25},{17,1},{25,9},{2,18},{10... | collective-permute-start | bytes 786440 | tf_op jit(solution)/shard_map/ppermute | solution.py:14
  218.7 3.4 copy-start.1
  222.1 7.3 %collective-permute-start.11 = (bf16[2,4,128,128]{3,2,1,0:T(8,128)(2,1)S(1)}, bf16[2,4,128,128]{3,2,1,0:T(8,128)(2,1)S(1)}, u32[]{:S(2)}, u32[]{:S(2)}) collective-permute-start(bf16[2,4,128,128]{3,2,1,0:T(8,128)(2,1)S(1)} %copy-done.1), channel_id=1, source_target_pairs={{0,24},{8,16},{16,8},{24,0},{1,25},{9,17},{17,9},{25,1},{2,26},{10... | collective-permute-start | bytes 786440 | tf_op jit(solution)/shard_map/ppermute | solution.py:14
  224.5 4.9 %copy-start.2 = (bf16[2,4,128,128]{3,2,1,0:T(8,128)(2,1)}, bf16[2,4,128,128]{3,2,1,0:T(8,128)(2,1)S(1)}, u32[]{:S(2)}) copy-start(bf16[2,4,128,128]{3,2,1,0:T(8,128)(2,1)S(1)} %collective-permute-done.9.rest_1_) | copy-start | bytes 786436
  224.5 4.9 %copy-start.3 = (bf16[2,4,128,128]{3,2,1,0:T(8,128)(2,1)}, bf16[2,4,128,128]{3,2,1,0:T(8,128)(2,1)S(1)}, u32[]{:S(2)}) copy-start(bf16[2,4,128,128]{3,2,1,0:T(8,128)(2,1)S(1)} %collective-permute-done.10.rest_2_) | copy-start | bytes 786436
  229.3 0.7 copy-start.4
  241.2 6.6 %copy-start = (bf16[3,1024,512]{2,1,0:T(8,128)(2,1)S(1)}, bf16[3,1024,512]{2,1,0:T(8,128)(2,1)}, u32[]{:S(2)}) copy-start(bf16[3,1024,512]{2,1,0:T(8,128)(2,1)} %shard_map.69.gradient_ref) | copy-start | bytes 9437188
  277.3 54.5 %collective-permute-start.15 = (bf16[3,768,512]{2,1,0:T(8,128)(2,1)}, bf16[3,768,512]{2,1,0:T(8,128)(2,1)S(1)}, u32[]{:S(2)}, u32[]{:S(2)}) collective-permute-start(bf16[3,768,512]{2,1,0:T(8,128)(2,1)} %convert_bitcast_fusion.2), channel_id=1, source_target_pairs={{0,16},{8,24},{16,0},{24,8},{1,17},{9,25},{17,1},{25,9},{2,18},{10... | collective-permute-start | bytes 7077896 | tf_op jit(solution)/shard_map/ppermute | solution.py:14
  278.9 60.3 %collective-permute-start.13 = (bf16[3,768,512]{2,1,0:T(8,128)(2,1)}, bf16[3,768,512]{2,1,0:T(8,128)(2,1)S(1)}, u32[]{:S(2)}, u32[]{:S(2)}) collective-permute-start(bf16[3,768,512]{2,1,0:T(8,128)(2,1)} %convert_bitcast_fusion.3), channel_id=1, source_target_pairs={{0,8},{8,0},{16,24},{24,16},{1,9},{9,1},{17,25},{25,17},{2,10},{10... | collective-permute-start | bytes 7077896 | tf_op jit(solution)/shard_map/ppermute | solution.py:14
  288.4 93.9 %collective-permute-start.17 = (bf16[3,768,512]{2,1,0:T(8,128)(2,1)S(1)}, bf16[3,768,512]{2,1,0:T(8,128)(2,1)S(1)}, u32[]{:S(2)}, u32[]{:S(2)}) collective-permute-start(bf16[3,768,512]{2,1,0:T(8,128)(2,1)S(1)} %convert_bitcast_fusion), channel_id=1, source_target_pairs={{0,16},{8,24},{16,0},{24,8},{1,17},{9,25},{17,1},{25,9},{2,18},{10... | collective-permute-start | bytes 7077896 | tf_op jit(solution)/shard_map/ppermute | solution.py:14
  332.5 54.3 %collective-permute-start.16 = (bf16[3,768,512]{2,1,0:T(8,128)(2,1)S(1)}, bf16[3,768,512]{2,1,0:T(8,128)(2,1)S(1)}, u32[]{:S(2)}, u32[]{:S(2)}) collective-permute-start(bf16[3,768,512]{2,1,0:T(8,128)(2,1)S(1)} %add_convert_fusion.1), channel_id=1, source_target_pairs={{0,8},{8,0},{16,24},{24,16},{1,9},{9,1},{17,25},{25,17},{2,10},{10... | collective-permute-start | bytes 7077896 | tf_op jit(solution)/shard_map/ppermute | solution.py:14
  337.7 90.0 %collective-permute-start.12 = (bf16[3,768,512]{2,1,0:T(8,128)(2,1)S(1)}, bf16[3,768,512]{2,1,0:T(8,128)(2,1)S(1)}, u32[]{:S(2)}, u32[]{:S(2)}) collective-permute-start(bf16[3,768,512]{2,1,0:T(8,128)(2,1)S(1)} %convert_bitcast_fusion.1), channel_id=1, source_target_pairs={{0,8},{8,0},{16,24},{24,16},{1,9},{9,1},{17,25},{25,17},{2,10},{10... | collective-permute-start | bytes 7077896 | tf_op jit(solution)/shard_map/ppermute | solution.py:14
  339.9 87.9 %collective-permute-start.14 = (bf16[3,768,512]{2,1,0:T(8,128)(2,1)S(1)}, bf16[3,768,512]{2,1,0:T(8,128)(2,1)S(1)}, u32[]{:S(2)}, u32[]{:S(2)}) collective-permute-start(bf16[3,768,512]{2,1,0:T(8,128)(2,1)S(1)} %add_convert_fusion.3), channel_id=1, source_target_pairs={{0,16},{8,24},{16,0},{24,8},{1,17},{9,25},{17,1},{25,9},{2,18},{10... | collective-permute-start | bytes 7077896 | tf_op jit(solution)/shard_map/ppermute | solution.py:14
Sparse Core Ops, SparseCore 0:
  9.6 119.4 all-gather.1
  277.4 129.5 reduce-scatter.1
